TPU v7x, 128 devices: a whole 4x4x4 slice. The times are simulated.
128 devices in a mesh: space: 16 (over x, z), mem: 8 (over y, core).
Axes of the slice: x: 4, y: 4, z: 4, core: 2. Of those that a mesh axis runs over, the one named last changes fastest.
Arguments:
- ensemble_state: bfloat16 [256, 1024, 256], P('mem', 'space'), may hold values from -6 to 6
- obs_ens: bfloat16 [256, 1024, 128], P('mem', 'space'), may hold values from -6 to 6
- innovation: float32 [1024, 128], P('space'), may hold values from -6 to 6
- obs_prec: float32 [1024, 128], P('space'), may hold values from 0.25 to 2
- block_list: int32 [1024, 8], P('space'), may hold values from 0 to 1023, as said below
- block_count: int32 [1024], P('space'), may hold values from 1 to 8
- loc_weight: float32 [1024, 8], P('space'), may hold values from 0.1 to 1
- prior_weight: float32 [1024, 256], P('space'), may hold values from 0.1 to 10, as said below
Outputs:
- analysis: bfloat16 [256, 1024, 256], P('mem', 'space')
Inputs may be any that keep to these rules, and one draw needn't show every extreme that they name: `block_list`: among the 64 entries of the regions r with the same r // 8, at most 6 name blocks b with the same b // 64, and exactly 6 do for one such value. `prior_weight`: Positive.
All inputs are finite; a program needn't handle non-finite values.
Results may differ from a plain program's by a relative error of at most 0.012.
Values may be sent and summed in bfloat16 or wider, within the bound.
A program may use at most 128 MiB of HBM per device.

v0:
```python
import jax
import jax.numpy as jnp
from jax import lax
from jax.sharding import PartitionSpec as P

INFLATION = 1.1


def transform(gram_blocks, projection, prior_rows):
    highest = lax.Precision.HIGHEST
    members = gram_blocks.shape[-1]
    shares = prior_rows / jnp.sum(prior_rows, axis=1, keepdims=True)
    root_q = jnp.sqrt(members * shares)
    left_term = jnp.einsum("rk,rkj->rj", shares, gram_blocks, precision=highest)
    centred = gram_blocks - left_term[:, None, :]
    right_term = jnp.einsum("rik,rk->ri", centred, shares, precision=highest)
    centred = centred - right_term[:, :, None]
    identity = jnp.eye(members, dtype=jnp.float32)
    system = (
        root_q[:, :, None] * centred * root_q[:, None, :] + (members - 1) / INFLATION * identity
    )
    vector = root_q * (projection - jnp.sum(shares * projection, axis=1, keepdims=True))
    factor = jnp.linalg.cholesky(system)
    inverse = jax.scipy.linalg.solve_triangular(
        factor, jnp.broadcast_to(identity, system.shape), lower=True
    )
    solved = jnp.einsum("rij,rj->ri", inverse, vector, precision=highest)
    weights = jnp.einsum("rji,rj->ri", inverse, solved, precision=highest)
    spread = jnp.sqrt(members - 1.0) * jnp.transpose(inverse, (0, 2, 1))
    mixing = root_q[:, :, None] * (weights[:, :, None] + spread)
    mixing = (
        mixing - shares[:, :, None] * jnp.sum(mixing, axis=1, keepdims=True) + shares[:, :, None]
    )
    return mixing


def body(
    ensemble_state, obs_ens, innovation, obs_prec, block_list, block_count, loc_weight, prior_weight
):
    spaces = lax.axis_size("space")
    mem_count = lax.axis_size("mem")
    members_dev = ensemble_state.shape[0]
    members = members_dev * mem_count
    regions_dev = ensemble_state.shape[1]
    group_size = regions_dev // mem_count
    blocks_dev = obs_ens.shape[1]
    obs_width = obs_ens.shape[2]
    slot_count = block_list.shape[1]
    entries = group_size * slot_count
    capacity = 3 * entries // (2 * spaces)
    mem_index = lax.axis_index("mem")
    first_row = mem_index * group_size
    block_ids = lax.dynamic_slice_in_dim(block_list, first_row, group_size, 0).reshape(entries)
    counts = lax.dynamic_slice_in_dim(block_count, first_row, group_size, 0)
    loc_rows = lax.dynamic_slice_in_dim(loc_weight, first_row, group_size, 0)
    prior_rows = lax.dynamic_slice_in_dim(prior_weight, first_row, group_size, 0)
    target = block_ids // blocks_dev
    local_ids = block_ids % blocks_dev
    onehot = (target[:, None] == jnp.arange(spaces, dtype=jnp.int32)[None, :]).astype(jnp.int32)
    slot_rank = jnp.sum(onehot * jnp.cumsum(onehot, axis=0), axis=1) - 1
    request_table = jnp.zeros((spaces, capacity), jnp.int32).at[target, slot_rank].set(local_ids)
    wanted = jnp.broadcast_to(request_table[:, None, :], (spaces, mem_count, capacity))
    wanted = wanted.reshape(spaces * mem_count, capacity)
    asked_ids = lax.all_to_all(wanted, ("space", "mem"), split_axis=0, concat_axis=0, tiled=True)
    outgoing = jnp.take(obs_ens, asked_ids, axis=1)
    arrived = lax.all_to_all(outgoing, ("space", "mem"), split_axis=1, concat_axis=1, tiled=True)
    arrived = arrived.reshape(members_dev, spaces, mem_count, capacity, obs_width)
    picked = arrived[:, target, :, slot_rank, :]
    picked = jnp.transpose(picked, (2, 1, 0, 3)).reshape(members, entries, obs_width)
    asked_grid = asked_ids.reshape(spaces, mem_count, capacity)
    from_peers = lax.dynamic_index_in_dim(asked_grid, mem_index, axis=1, keepdims=False)
    error_prec = jnp.take(obs_prec, from_peers, axis=0)
    error_innov = jnp.take(innovation, from_peers, axis=0)
    got_prec, got_innov = (
        lax.all_to_all(error_prec, "space", split_axis=0, concat_axis=0, tiled=True),
        lax.all_to_all(error_innov, "space", split_axis=0, concat_axis=0, tiled=True),
    )
    prec_rows = got_prec[target, slot_rank]
    innov_rows = got_innov[target, slot_rank]
    active = (jnp.arange(slot_count, dtype=jnp.int32)[None, :] < counts[:, None]).astype(
        jnp.float32
    )
    obs_weight = (active * loc_rows).reshape(entries)[:, None] * prec_rows
    obs_scale = jnp.sqrt(obs_weight)
    scaled = (picked.astype(jnp.float32) * obs_scale[None]).astype(jnp.bfloat16)
    shaped = scaled.reshape(members, group_size, slot_count, obs_width)
    gram_blocks = jnp.einsum("krlo,jrlo->rkj", shaped, shaped, preferred_element_type=jnp.float32)
    weighted_innov = (obs_scale * innov_rows).reshape(group_size, slot_count, obs_width)
    projection = jnp.einsum(
        "krlo,rlo->rk", shaped, weighted_innov, preferred_element_type=jnp.float32
    )
    mixing = transform(gram_blocks, projection, prior_rows)
    mix_high = mixing.astype(jnp.bfloat16)
    mix_low = (mixing - mix_high.astype(jnp.float32)).astype(jnp.bfloat16)
    mix_parts = jnp.concatenate([mix_high, mix_low], axis=2)
    region_states = lax.all_to_all(ensemble_state, "mem", split_axis=1, concat_axis=0, tiled=True)
    both_parts = jnp.einsum(
        "krp,rkj->jrp", region_states, mix_parts, preferred_element_type=jnp.float32
    )
    updated = (both_parts[:members] + both_parts[members:]).astype(jnp.bfloat16)
    return lax.all_to_all(updated, "mem", split_axis=0, concat_axis=1, tiled=True)


def solution(mesh):
    return jax.shard_map(
        body,
        mesh=mesh,
        in_specs=(
            P("mem", "space", None),
            P("mem", "space", None),
            P("space", None),
            P("space", None),
            P("space", None),
            P("space"),
            P("space", None),
            P("space", None),
        ),
        out_specs=P("mem", "space", None),
        check_vma=False,
    )
```

profile of v0, /device:TPU:1, one launch (start us, length us, event | category | flops | bytes accessed | tf_op | source)
XLA Modules:
  0.0 712.9 jit_solution(11391945641153206880)
XLA Ops:
  0.0 0.9 constant_dynamic-slice_fusion.2
  1.3 0.2 select_reduce_fusion.2
  1.6 3.5 scatter_fusion
  5.1 0.6 broadcast_in_dim.30.clone
  5.8 11.5 %all-to-all-start = ((s32[128,1,6]{2,1,0:T(1,128)}), s32[128,1,6]{2,1,0:T(1,128)S(1)}, u32[]{:S(2)}, u32[]{:S(2)}) async-start(s32[128,1,6]{2,1,0:T(1,128)} %bitcast.3), calls=%async_computation | async-start | bytes 131072 | tf_op jit(solution)/shard_map/all_to_all | solution.py:64
  17.3 9.4 %all-to-all-done = s32[128,1,6]{2,1,0:T(1,128)S(1)} async-done(((s32[128,1,6]{2,1,0:T(1,128)}), s32[128,1,6]{2,1,0:T(1,128)S(1)}, u32[]{:S(2)}, u32[]{:S(2)}) %all-to-all-start) | async-done | bytes 3104 | tf_op jit(solution)/shard_map/all_to_all | solution.py:64
  27.0 1.4 gather_fusion.4
  28.4 0.6 gather_fusion.5
  29.1 0.7 broadcast_select_fusion.1
  29.8 9.7 %all_to_all.66 = f32[16,6,128]{2,1,0:T(8,128)S(1)} all-to-all(f32[16,6,128]{2,1,0:T(8,128)S(1)} %get-tuple-element.39), channel_id=1, replica_groups=mesh['space'=16,'mem'=8] {'space'}, dimensions={0} | all-to-all | bytes 98304 | tf_op jit(solution)/shard_map/all_to_all | solution.py:75
  39.6 3.5 all-to-all-start.3
  43.1 1.6 copy.140
  44.6 4.9 all-to-all-done.3
  49.5 6.6 all-to-all-start.4
  56.3 29.1 %gather_fusion = bf16[768,32,128]{2,0,1:T(8,128)(2,1)} fusion(bf16[32,64,128]{2,1,0:T(8,128)(2,1)S(1)} %copy-done, s32[1024]{0:T(1024)S(1)} %pad_clamp_fusion.1), kind=kCustom, calls=%fused_computation.2 | custom fusion | bytes 12585984 | tf_op jit(solution)/shard_map/jit(_take)/gather | solution.py:65
  85.4 6.8 copy.116
  92.3 3.5 select_bitcast_fusion
  95.8 6.3 all-to-all-start.1
  102.5 0.8 dynamic-slice_reduce_fusion
  103.5 0.9 gather_fusion.2
  104.4 0.9 gather_fusion.3
  105.4 1.1 copy.141
  106.5 71.5 %all-to-all-done.1 = bf16[32,128,6,128]{3,0,2,1:T(8,128)(2,1)} async-done(((bf16[32,128,6,128]{3,0,2,1:T(8,128)(2,1)}), bf16[32,128,6,128]{3,0,2,1:T(8,128)(2,1)}, u32[]{:S(2)}, u32[]{:S(2)}) %all-to-all-start.1) | async-done | bytes 6291488 | tf_op jit(solution)/shard_map/all_to_all | solution.py:66
  178.0 9.5 %copy.118 = bf16[32,16,8,6,128]{4,2,3,1,0:T(8,128)(2,1)} copy(bf16[32,16,8,6,128]{4,0,3,2,1:T(8,128)(2,1)} %bitcast.8) | data formatting | bytes 12582912 | tf_op jit(solution)/shard_map/reshape | solution.py:67
  187.4 6.6 gather_fusion.1
  194.1 3.3 convert_bitcast_fusion
  197.3 13.6 %copy.119 = f32[8,32,64,128]{3,2,1,0:T(8,128)S(1)} copy(f32[8,32,64,128]{3,0,1,2:T(8,128)S(1)} %convert_bitcast_fusion) | data formatting | bytes 16777216 | tf_op jit(solution)/shard_map/convert_element_type | solution.py:85
  210.9 1.2 multiply_convert_fusion
  212.1 5.8 fusion.15
  217.9 2.3 fusion.1
  220.2 1.9 copy.127
  222.1 0.9 fusion.39
  223.1 2.7 fusion.45
  225.8 1.3 fusion.13
  227.2 1.7 fusion.20
  228.8 2.9 copy.129
  231.7 2.2 fusion.12
  233.9 1.3 copy-done.5
  235.3 93.8 %custom-call.17 = f32[8,128,128]{2,1,0:T(8,128)S(1)} custom-call(f32[8,128,128]{2,1,0:T(8,128)S(1)} %cholesky.122), custom_call_target="Cholesky" | custom-call | tf_op jit(solution)/shard_map/jit(cholesky)/cholesky | solution.py:23
  329.1 0.2 cholesky.117
  329.3 79.2 %custom-call.18 = f32[8,1,128,128]{2,3,1,0:T(8,128)} custom-call(f32[8,1,128,128]{3,2,1,0:T(8,128)S(1)} %select_bitcast_fusion.1), custom_call_target="InvertDiagBlocksLowerTriangular" | custom-call | tf_op jit(solution)/shard_map/jit(cholesky)/cholesky | solution.py:23
  408.5 1.8 constant_dynamic-update-slice_fusion.1
  410.4 3.1 convolution_subtract_fusion.1
  413.4 94.8 %custom-call.19 = f32[8,128,128]{2,1,0:T(8,128)S(1)} custom-call(f32[8,128,128]{2,1,0:T(8,128)} %convolution_subtract_fusion.1), custom_call_target="Cholesky" | custom-call | tf_op jit(solution)/shard_map/jit(cholesky)/cholesky | solution.py:23
  508.5 1.2 copy-done.4
  509.7 1.9 select_select_fusion
  511.7 5.8 while.1
  511.7 0.6 fusion.66
  512.3 2.3 bitcast_dynamic-update-slice_fusion.2
  514.6 0.6 fusion.66
  515.2 2.2 bitcast_dynamic-update-slice_fusion.2
  517.4 158.6 %custom-call.20 = f32[8,2,128,128]{2,3,1,0:T(8,128)} custom-call(f32[8,2,128,128]{3,2,1,0:T(8,128)} %bitcast.159), custom_call_target="InvertDiagBlocksLowerTriangular" | custom-call | tf_op jit(solution)/shard_map/jit(_solve_triangular)/vmap()/triangular_solve | solution.py:24
  676.1 3.1 fusion.29
  679.1 2.6 copy.135
  681.7 2.4 convolution_subtract_fusion
  684.1 2.0 fusion.28
  686.1 1.2 fusion.26
  687.3 1.8 fusion.25
  689.2 1.7 subtract_convert_fusion
  690.9 0.8 convolution_bitcast_fusion
  691.7 0.2 fusion.5
  692.0 0.6 copy.143
  692.5 18.8 %all_to_all.67 = bf16[256,8,256]{2,1,0:T(8,128)(2,1)S(1)} all-to-all(bf16[256,8,256]{2,1,0:T(8,128)(2,1)S(1)} %copy.143), channel_id=1, replica_groups=mesh['space'=16,'mem'=8] {'mem'}, dimensions={0} | all-to-all | bytes 2097152 | tf_op jit(solution)/shard_map/all_to_all | solution.py:101
  711.4 1.1 copy.196
  (74 shorter events, 2.2 us)
Async XLA Ops:
  0.0 56.3 %copy-start = (bf16[32,64,128]{2,1,0:T(8,128)(2,1)S(1)}, bf16[32,64,128]{2,1,0:T(8,128)(2,1)}, u32[]{:S(2)}) copy-start(bf16[32,64,128]{2,1,0:T(8,128)(2,1)} %param.11) | copy-start | bytes 1572868
  0.0 28.4 %copy-start.3 = (f32[64,128]{1,0:T(8,128)S(1)}, f32[64,128]{1,0:T(8,128)}, u32[]{:S(2)}) copy-start(f32[64,128]{1,0:T(8,128)} %param.12) | copy-start | bytes 98308
  0.0 43.0 %copy-start.8 = (bf16[32,64,256]{2,1,0:T(8,128)(2,1)S(1)}, bf16[32,64,256]{2,1,0:T(8,128)(2,1)}, u32[]{:S(2)}) copy-start(bf16[32,64,256]{2,1,0:T(8,128)(2,1)} %param.10) | copy-start | bytes 3145732
  5.8 20.9 %all-to-all-start = ((s32[128,1,6]{2,1,0:T(1,128)}), s32[128,1,6]{2,1,0:T(1,128)S(1)}, u32[]{:S(2)}, u32[]{:S(2)}) async-start(s32[128,1,6]{2,1,0:T(1,128)} %bitcast.3), calls=%async_computation | async-start | bytes 131072 | tf_op jit(solution)/shard_map/all_to_all | solution.py:64
  39.6 10.0 %all-to-all-start.3 = ((f32[16,6,128]{2,1,0:T(8,128)}), f32[16,6,128]{2,1,0:T(8,128)S(1)}, u32[]{:S(2)}, u32[]{:S(2)}) async-start(f32[16,6,128]{2,1,0:T(8,128)} %get-tuple-element.40), calls=%async_computation.3 | async-start | bytes 131072 | tf_op jit(solution)/shard_map/all_to_all | solution.py:76
  49.5 46.3 %all-to-all-start.4 = ((bf16[32,64,256]{2,0,1:T(8,128)(2,1)}), bf16[32,64,256]{2,0,1:T(8,128)(2,1)S(1)}, u32[]{:S(2)}, u32[]{:S(2)}) async-start(bf16[32,64,256]{2,0,1:T(8,128)(2,1)} %copy.140), calls=%async_computation.4 | async-start | bytes 2097152 | tf_op jit(solution)/shard_map/all_to_all | solution.py:96
  95.8 6.4 copy-start.10
  95.8 6.4 copy-start.9
  95.8 82.1 %all-to-all-start.1 = ((bf16[32,128,6,128]{3,0,2,1:T(8,128)(2,1)}), bf16[32,128,6,128]{3,0,2,1:T(8,128)(2,1)}, u32[]{:S(2)}, u32[]{:S(2)}) async-start(bf16[32,128,6,128]{3,0,2,1:T(8,128)(2,1)} %select_bitcast_fusion), calls=%async_computation.1 | async-start | bytes 12582912 | tf_op jit(solution)/shard_map/all_to_all | solution.py:66
  233.9 1.3 copy-start.5
  508.3 1.3 copy-start.4
  681.7 2.4 copy-start.7
  681.7 4.4 copy-start.2
  689.2 1.7 copy-start.6
  691.9 20.5 %copy-start.1 = (bf16[32,64,128]{2,1,0:T(8,128)(2,1)S(1)}, bf16[32,64,128]{2,1,0:T(8,128)(2,1)}, u32[]{:S(2)}) copy-start(bf16[32,64,128]{2,1,0:T(8,128)(2,1)} %param.11) | copy-start | bytes 1572868
where the time goes:
time: 722 us; the launch traced here: 713 us
  other arithmetic  446 us (62%)
  local copies, waits for them, and re-layouts  95.8 us (13%)
  waiting for transfers between devices  85.8 us (12%)
  blocking collectives  28.5 us (4%)
  matrix products  28.4 us (4%)
  starting transfers between devices  27.9 us (4%)
    another operation x9, other arithmetic, transform(): factor = jnp.linalg.cholesky(system)  268 us
    another operation x4, other arithmetic, transform(): jax.scipy.linalg.solve_triangular(factor, jnp.broadcast_to(identity, syst...  161 us
    all_to_all x1, waiting for transfers between devices, body(): lax.all_to_all(outgoing, ('space', 'mem'), split_axis=1, concat_axis=1, t...  71.5 us
    gather x2, local copies, waits for them, and re-layouts, body(): outgoing = jnp.take(obs_ens, asked_ids, axis=1)  35.9 us
    all_to_all x1, blocking collectives, body(): lax.all_to_all(updated, 'mem', split_axis=0, concat_axis=1, tiled=True)  18.8 us
  transfers between devices with their start and end apart: 4, of which 3 were waited for; matrix products, arithmetic and copies ran while one was open for 6% of the time, Pallas kernels for 0%

commit v1 on v0

v1 whole, which is shorter than its diff:
```python
import functools
import math

import jax
import jax.numpy as jnp
from jax import lax
from jax.experimental import pallas as pl
from jax.experimental.pallas import tpu as pltpu
from jax.sharding import PartitionSpec as P

INFLATION = 1.1
HIGHEST = lax.Precision.HIGHEST
F32 = jnp.float32
BF16 = jnp.bfloat16


def dot(a, b, dims, precision=None):
    return lax.dot_general(a, b, (dims, ((), ())), precision=precision, preferred_element_type=F32)


def split(x):
    high = x.astype(BF16)
    return high, (x - high.astype(F32)).astype(BF16)


def dot_f32(a, b, dims, mode):
    if mode == 6:
        return dot(a, b, dims, HIGHEST)
    ah, al = split(a)
    bh, bl = split(b)
    return dot(ah, bh, dims) + (dot(ah, bl, dims) + dot(al, bh, dims))


def eliminate(rows, group):
    count = len(rows)
    rows = list(rows)

    def lane(x, i):
        return jnp.broadcast_to(x[:, i : i + 1], x.shape)

    for k in range(0, count, group):
        small = {(a, b): lane(rows[k + a], k + b) for a in range(group) for b in range(a, group)}
        for a in range(group):
            root = lax.rsqrt(small[a, a])
            upper = {b: small[a, b] * root for b in range(a + 1, group)}
            rows[k + a] = rows[k + a] * root
            for c in range(a + 1, group):
                rows[k + c] = rows[k + c] - upper[c] * rows[k + a]
                for b in range(c, group):
                    small[c, b] = small[c, b] - upper[c] * upper[b]
        for i in range(k + group, count):
            for a in range(group):
                rows[i] = rows[i] - lane(rows[k + a], i) * rows[k + a]
    return rows


def analyse(
    me, list_ref, count_ref, loc_ref, table_ref, prior_ref, obs_ref, state_ref, out_ref,
    seen, extra, system, diag, inv, qcol, *, nb, group, mode,
):
    mems, entries, members_dev, width = obs_ref.shape
    members = mems * members_dev
    slots = list_ref.shape[1]
    regions = entries // slots
    first = me * regions
    shares_all = prior_ref[pl.ds(first, regions), :]
    shares_all = shares_all / jnp.sum(shares_all, axis=1, keepdims=True)
    root_all = jnp.sqrt(members * shares_all)
    root_t = jnp.transpose(root_all)
    for r in range(regions):
        qcol[r] = jnp.broadcast_to(root_t[:, r : r + 1], (members, 128))
    extra[...] = jnp.zeros_like(extra)
    row_id = lax.broadcasted_iota(jnp.int32, (members, members), 0)
    col_id = lax.broadcasted_iota(jnp.int32, (members, members), 1)
    vec_scr = []

    def shares_of(r):
        s = prior_ref[pl.ds(first + r, 1), :]
        return s / jnp.sum(s, axis=1, keepdims=True)

    def build(r, carry):
        row = first + r
        for l in range(slots):
            block = list_ref[row, l]
            both = table_ref[pl.ds(block, 1), :]
            live = jnp.where(l < count_ref[row], loc_ref[row, l], 0.0)
            scale = jnp.sqrt(live * both[:, :width])
            picked = obs_ref[:, r * slots + l].reshape(members, width).astype(F32)
            cols = slice(l * width, (l + 1) * width)
            seen[:, cols] = (picked * scale).astype(BF16)
            high, low = split(scale * both[:, width:])
            extra[0:1, cols] = high.astype(F32)
            extra[1:2, cols] = low.astype(F32)
        all_seen = seen[...]
        gram = dot(all_seen, all_seen, ((1,), (1,)))
        proj = dot(extra[...].astype(BF16), all_seen, ((1,), (1,)))
        proj = proj[0:1] + proj[1:2]
        shares = shares_of(r)
        root = jnp.sqrt(members * shares)
        left = dot(jnp.broadcast_to(shares, (8, members)), gram, ((1,), (0,)), HIGHEST)[0:1]
        centred = gram - left
        centred = centred - jnp.sum(centred * shares, axis=1, keepdims=True)
        q = jnp.concatenate([qcol[r]] * (members // 128), axis=1)
        full = q * centred * root + jnp.where(row_id == col_id, (members - 1) / INFLATION, 0.0)
        at = pl.ds(pl.multiple_of(r * members, members), members)
        for half in range(members // 128):
            system[half, at, :] = full[:, half * 128 : (half + 1) * 128]
        vector = root * (proj - jnp.sum(shares * proj, axis=1, keepdims=True))
        inv[pl.ds(r, 1), :] = vector
        return carry

    lax.fori_loop(0, regions, build, 0)

    lane_id = lax.broadcasted_iota(jnp.int32, (regions, 128), 1)
    halves = members // 128
    per_half = 128 // nb
    for b in range(members // nb):
        half, place = b // per_half, (b % per_half) * nb
        def factor(_, carry):
            rows = []
            for i in range(nb):
                x = system[half, pl.ds(b * nb + i, regions, stride=members), :]
                if place:
                    x = pltpu.roll(x, 128 - place, 1)
                rows.append(jnp.where(lane_id < nb, x, jnp.where(lane_id == nb + i, 1.0, 0.0)))
            rows = eliminate(rows, group)
            for i in range(nb):
                diag[pl.ds(i, regions, stride=nb), :] = rows[i]
            return carry

        factor(0, 0)

        def sweep(r, carry):
            start = r * members + b * nb
            here = pl.ds(pl.multiple_of(start, nb), nb)
            small = diag[pl.ds(pl.multiple_of(r * nb, nb), nb), :][:, nb : 2 * nb]
            band = jnp.concatenate([system[h, here, :] for h in range(halves)], axis=1)
            ids = lax.broadcasted_iota(jnp.int32, (nb, members), 1)
            rid = lax.broadcasted_iota(jnp.int32, (nb, members), 0)
            mine = (ids >= b * nb) & (ids < (b + 1) * nb)
            band = jnp.where(mine, jnp.where(ids - b * nb == rid, 1.0, 0.0), band)
            done = dot_f32(small, band, ((1,), (0,)), mode)
            kept = jnp.where(ids < (b + 1) * nb, done, 0.0)
            for h in range(halves):
                system[h, here, :] = kept[:, h * 128 : (h + 1) * 128]
            rest = members - (b + 1) * nb
            if rest:
                below = pl.ds(pl.multiple_of(start + nb, nb), rest)
                change = dot_f32(done[:, (b + 1) * nb :], done, ((0,), (0,)), mode)
                for h in range(halves):
                    old = system[h, below, :]
                    if h == half:
                        hl = lax.broadcasted_iota(jnp.int32, (rest, 128), 1)
                        old = jnp.where((hl >= place) & (hl < place + nb), 0.0, old)
                    system[h, below, :] = old - change[:, h * 128 : (h + 1) * 128]
            return carry

        lax.fori_loop(0, regions, sweep, 0)

    def finish(r, carry):
        at = pl.ds(pl.multiple_of(r * members, members), members)
        inverse = jnp.concatenate([system[h, at, :] for h in range(halves)], axis=1)
        shares = shares_of(r)
        root = jnp.sqrt(members * shares)
        solved = jnp.sum(inverse * inv[pl.ds(r, 1), :], axis=1, keepdims=True)
        weights = jnp.sum(inverse * solved, axis=0, keepdims=True)
        mixing = root * (weights + math.sqrt(members - 1.0) * inverse)
        mixing = mixing - jnp.sum(mixing, axis=1, keepdims=True) * shares + shares
        high, low = split(mixing)
        states = state_ref[:, r].reshape(members, state_ref.shape[3])
        done = dot(high, states, ((1,), (0,))) + dot(low, states, ((1,), (0,)))
        out_ref[:, r] = done.astype(BF16).reshape(mems, members_dev, state_ref.shape[3])
        return carry

    lax.fori_loop(0, regions, finish, 0)


def analysis_scratch(members, regions, slots, width, nb):
    return [
        pltpu.VMEM((members, slots * width), BF16),
        pltpu.VMEM((16, slots * width), F32),
        pltpu.VMEM((members // 128, regions * members, 128), F32),
        pltpu.VMEM((regions * nb, 128), F32),
        pltpu.VMEM((regions, members), F32),
        pltpu.VMEM((regions, members, 128), F32),
    ]


def collect(list_ref, all_ref, out_ref):
    rows, slots = list_ref.shape

    def one(r, carry):
        for l in range(slots):
            out_ref[r * slots + l] = all_ref[list_ref[r, l]]
        return carry

    lax.fori_loop(0, rows, one, 0)


def analyse_here(*refs, nb, group, mode):
    analyse(lax.axis_index("mem"), *refs, nb=nb, group=group, mode=mode)


SMEM = pl.BlockSpec(memory_space=pltpu.SMEM)
VMEM = pl.BlockSpec(memory_space=pltpu.VMEM)


def body(
    ensemble_state, obs_ens, innovation, obs_prec, block_list, block_count, loc_weight, prior_weight
):
    mems = lax.axis_size("mem")
    members_dev, regions_dev, p_size = ensemble_state.shape
    width = obs_ens.shape[2]
    slots = block_list.shape[1]
    regions = regions_dev // mems
    entries = regions * slots
    members = members_dev * mems
    params = pltpu.CompilerParams(vmem_limit_bytes=56 << 20)

    table = jnp.concatenate([obs_prec, innovation], axis=1)
    table = lax.all_gather(table, "space", axis=0, tiled=True)
    blocks = jnp.transpose(obs_ens, (1, 0, 2))
    blocks = lax.all_gather(blocks, "space", axis=0, tiled=True)
    states = jnp.transpose(ensemble_state, (1, 0, 2))
    states = lax.all_to_all(states, "mem", split_axis=0, concat_axis=0, tiled=True)
    states = states.reshape(mems, regions, members_dev, p_size)
    listed = pl.pallas_call(
        collect,
        in_specs=[SMEM, VMEM],
        out_specs=VMEM,
        out_shape=jax.ShapeDtypeStruct((regions_dev * slots, members_dev, width), BF16),
        compiler_params=params,
    )(block_list, blocks)
    seen = lax.all_to_all(listed, "mem", split_axis=0, concat_axis=0, tiled=True)
    seen = seen.reshape(mems, entries, members_dev, width)
    nb = 64
    updated = pl.pallas_call(
        functools.partial(analyse_here, nb=nb, group=8, mode=6),
        in_specs=[SMEM, SMEM, SMEM, VMEM, VMEM, VMEM, VMEM],
        out_specs=VMEM,
        out_shape=jax.ShapeDtypeStruct((mems, regions, members_dev, p_size), BF16),
        scratch_shapes=analysis_scratch(members, regions, slots, width, nb),
        compiler_params=params,
    )(block_list, block_count, loc_weight, table, prior_weight, seen, states)
    updated = updated.reshape(regions_dev, members_dev, p_size)
    updated = lax.all_to_all(updated, "mem", split_axis=0, concat_axis=0, tiled=True)
    return jnp.transpose(updated, (1, 0, 2))


def solution(mesh):
    return jax.shard_map(
        body,
        mesh=mesh,
        in_specs=(
            P("mem", "space", None),
            P("mem", "space", None),
            P("space", None),
            P("space", None),
            P("space", None),
            P("space"),
            P("space", None),
            P("space", None),
        ),
        out_specs=P("mem", "space", None),
        check_vma=False,
    )
```

time: 722 us -> 223 us (0.31); the launches traced: 713 us -> 223 us
  other arithmetic: 446 us -> 0.63 us
  local copies, waits for them, and re-layouts: 95.8 us -> 7.96 us
  Pallas kernels: 0 us -> 57.1 us
  matrix products: 28.4 us -> 0 us
  waiting for transfers between devices: 85.8 us -> 113 us
  starting transfers between devices: 27.9 us -> 11.2 us
  between operations: 0.91 us -> 13.4 us
  blocking collectives: 28.5 us -> 19.4 us
    another operation x14 -> x0, other arithmetic: 429 us -> none  [the longest x9 268 us: transform(): factor = jnp.linalg.cholesky(system)]
    all_gather x0 -> x2, waiting for transfers between devices: none -> 108 us  [the longest x1 65.4 us: body(): blocks = lax.all_gather(blocks, 'space', axis=0, tiled=True)]
    all_to_all x4 -> x2, waiting for transfers between devices: 85.8 us -> 4.82 us  [the longest x1 4.81 us: body(): lax.all_to_all(listed, 'mem', split_axis=0, concat_axis=0, tiled=True)]
    pallas_call x0 -> x2, Pallas kernels: none -> 57.1 us  [the longest x1 50.9 us: body(): pl.pallas_call(functools.partial(analyse_here, nb=nb, group=8, mode=6), i...]
    gather x9 -> x0, local copies, waits for them, and re-layouts: 46.3 us -> none  [the longest x2 35.9 us: body(): outgoing = jnp.take(obs_ens, asked_ids, axis=1)]
    all_to_all x4 -> x2, starting transfers between devices: 27.9 us -> 11.2 us  [the longest x1 5.97 us: body(): lax.all_to_all(states, 'mem', split_axis=0, concat_axis=0, tiled=True)]
    dot_general x7 -> x0, matrix products: 16 us -> none  [the longest x1 5.83 us: body(): jnp.einsum('krlo,jrlo->rkj', shaped, shaped, preferred_element_type=jnp.f...]
    convert_element_type x2 -> x0, local copies, waits for them, and re-layouts: 14.2 us -> none  [the longest x1 13.6 us: body(): scaled = (picked.astype(jnp.float32) * obs_scale[None]).astype(jnp.bfloat16)]
  transfers between devices with their start and end apart: 4 -> 4, of which waited for: 3 -> 3; matrix products, arithmetic and copies ran while one was open for 6% -> 2% of each run, Pallas kernels for 0% -> 3%
where the time goes in v1:
time: 223 us
  waiting for transfers between devices  113 us (51%)
  Pallas kernels  57.1 us (26%)
  blocking collectives  19.4 us (9%)
  between operations  13.4 us (6%)
  starting transfers between devices  11.2 us (5%)
  local copies, waits for them, and re-layouts  7.96 us (4%)
    all_gather x1, waiting for transfers between devices, body(): blocks = lax.all_gather(blocks, 'space', axis=0, tiled=True)  65.4 us
    pallas_call x1, Pallas kernels, body(): pl.pallas_call(functools.partial(analyse_here, nb=nb, group=8, mode=6), i...  50.9 us
    all_gather x1, waiting for transfers between devices, body(): table = lax.all_gather(table, 'space', axis=0, tiled=True)  42.7 us
    all_to_all x1, blocking collectives, body(): lax.all_to_all(updated, 'mem', split_axis=0, concat_axis=0, tiled=True)  19.4 us
    unnamed x14, local copies, waits for them, and re-layouts  6.4 us
    pallas_call x1, Pallas kernels, body(): pl.pallas_call(collect, in_specs=[SMEM, VMEM], out_specs=VMEM, out_shape=...  6.23 us
    all_to_all x1, starting transfers between devices, body(): lax.all_to_all(states, 'mem', split_axis=0, concat_axis=0, tiled=True)  5.97 us
    all_to_all x1, starting transfers between devices, body(): lax.all_to_all(listed, 'mem', split_axis=0, concat_axis=0, tiled=True)  5.24 us
  transfers between devices with their start and end apart: 4, of which 3 were waited for; matrix products, arithmetic and copies ran while one was open for 2% of the time, Pallas kernels for 3%

profile of v1, /device:TPU:1, one launch (start us, length us, event | category | flops | bytes accessed | tf_op | source)
XLA Modules:
  0.0 222.7 jit_solution(5578957781838979350)
XLA Ops:
  6.5 0.0 copy-start.3
  6.5 0.0 all-gather.5.cloned.1.call-start
  6.5 2.2 copy.24
  8.8 0.0 all-gather.5.cloned.1.call-update
  8.8 2.8 %copy.23 = bf16[32,64,256]{2,0,1:T(8,128)(2,1)} copy(bf16[32,64,256]{2,1,0:T(8,128)(2,1)} %param.8) | data formatting | bytes 2097152 | tf_op args[0]
  11.6 6.0 %all-to-all-start.1 = ((bf16[64,32,256]{2,1,0:T(8,128)(2,1)}), bf16[64,32,256]{2,1,0:T(8,128)(2,1)S(1)}, u32[]{:S(2)}, u32[]{:S(2)}) async-start(bf16[64,32,256]{2,1,0:T(8,128)(2,1)} %bitcast.8), calls=%async_computation.1 | async-start | bytes 2097152 | tf_op jit(solution)/shard_map/all_to_all | solution.py:225
  17.5 0.0 copy-done.3
  17.5 0.7 copy.18.list_ref.refs_0_
  18.2 65.4 %all-gather.5.cloned.1.call-done.all_ref = bf16[1024,32,128]{2,1,0:T(8,128)(2,1)} async-done(((bf16[64,32,128]{2,1,0:T(8,128)(2,1)}), bf16[1024,32,128]{2,1,0:T(8,128)(2,1)}) %all-gather.5.cloned.1.call-update) | async-done | bytes 8388624 | tf_op jit(solution)/shard_map/all_gather | solution.py:223
  83.6 6.2 %shard_map.82 = bf16[512,32,128]{2,1,0:T(8,128)(2,1)} custom-call(s32[64,8]{1,0:T(8,128)} %copy.18.list_ref.refs_0_, bf16[1024,32,128]{2,1,0:T(8,128)(2,1)} %all-gather.5.cloned.1.call-done.all_ref), custom_call_target="tpu_custom_call" | custom-call | tf_op jit(solution)/shard_map/pallas_call | solution.py:227
  89.8 0.0 copy-start.1
  89.8 0.0 copy-start.2
  89.8 0.0 copy-start.4
  89.8 0.0 all-to-all-done.1
  89.8 0.0 copy-start
  89.9 5.2 %all-to-all-start = ((bf16[512,32,128]{2,1,0:T(8,128)(2,1)}), bf16[512,32,128]{2,1,0:T(8,128)(2,1)}, u32[]{:S(2)}, u32[]{:S(2)}) async-start(bf16[512,32,128]{2,1,0:T(8,128)(2,1)} %shard_map.82), calls=%async_computation | async-start | bytes 8388608 | tf_op jit(solution)/shard_map/all_to_all | solution.py:234
  95.1 0.0 all-gather.3.cloned.1.call-start
  95.1 0.0 copy-done.1
  95.1 0.0 copy-done.2
  95.1 0.6 pad_maximum_fusion
  95.7 0.0 copy-done
  95.7 0.1 all-gather.3.cloned.1.call-update
  95.8 0.0 copy-done.4
  95.8 0.7 copy.19.refs_2_
  96.5 42.7 %all-gather.3.cloned.1.call-done.refs_3_ = f32[1024,256]{1,0:T(8,128)} async-done(((f32[64,256]{1,0:T(8,128)}), f32[1024,256]{1,0:T(8,128)}) %all-gather.3.cloned.1.call-update) | async-done | bytes 1048592 | tf_op jit(solution)/shard_map/all_gather | solution.py:221
  139.2 4.8 %all-to-all-done = bf16[512,32,128]{2,1,0:T(8,128)(2,1)} async-done(((bf16[512,32,128]{2,1,0:T(8,128)(2,1)}), bf16[512,32,128]{2,1,0:T(8,128)(2,1)}, u32[]{:S(2)}, u32[]{:S(2)}) %all-to-all-start) | async-done | bytes 4194336 | tf_op jit(solution)/shard_map/all_to_all | solution.py:234
  144.0 50.9 %shard_map.83 = bf16[8,8,32,256]{3,2,1,0:T(8,128)(2,1)} custom-call(s32[64,8]{1,0:T(8,128)} %copy.18.list_ref.refs_0_, s32[64]{0:T(128)} %refs_1_.1, f32[64,8]{1,0:T(8,128)} %copy.19.refs_2_, f32[1024,256]{1,0:T(8,128)} %all-gather.3.cloned.1.call-done.refs_3_, f32[64,256]{1,0:T(8,128)} %refs_4_.1, bf16[8,64,32,128]{3,2,1,0:T(8,128)(2,1)} %bitcast.1.refs_5_, ...), custom_call_target="tpu_custom_call" | custom-call | tf_op jit(solution)/shard_map/pallas_call | solution.py:237
  194.9 19.4 %all_to_all.15 = bf16[64,32,256]{2,1,0:T(8,128)(2,1)S(1)} all-to-all(bf16[64,32,256]{2,1,0:T(8,128)(2,1)} %bitcast.12), channel_id=1, replica_groups=mesh['space'=16,'mem'=8] {'mem'}, dimensions={0} | all-to-all | bytes 2097152 | tf_op jit(solution)/shard_map/all_to_all | solution.py:246
  214.3 1.6 copy.20
Async XLA Ops:
  6.5 11.0 %copy-start.3 = (s32[64,8]{0,1:T(8,128)S(1)}, s32[64,8]{0,1:T(8,128)}, u32[]{:S(2)}) copy-start(s32[64,8]{0,1:T(8,128)} %param.12) | copy-start | bytes 6148
  6.5 77.1 %all-gather.5.cloned.1.call-start = ((), (), s32[]{:S(2)}) async-start(), calls=%async_computation.4 | async-start | bytes 8912896 | tf_op jit(solution)/shard_map/all_gather | solution.py:223
  11.6 78.3 %all-to-all-start.1 = ((bf16[64,32,256]{2,1,0:T(8,128)(2,1)}), bf16[64,32,256]{2,1,0:T(8,128)(2,1)S(1)}, u32[]{:S(2)}, u32[]{:S(2)}) async-start(bf16[64,32,256]{2,1,0:T(8,128)(2,1)} %bitcast.8), calls=%async_computation.1 | async-start | bytes 2097152 | tf_op jit(solution)/shard_map/all_to_all | solution.py:225
  89.8 5.3 %copy-start.1 = (f32[64,128]{1,0:T(8,128)S(1)}, f32[64,128]{1,0:T(8,128)}, u32[]{:S(2)}) copy-start(f32[64,128]{1,0:T(8,128)} %param.10) | copy-start | bytes 98308
  89.8 5.3 %copy-start.2 = (f32[64,128]{1,0:T(8,128)S(1)}, f32[64,128]{1,0:T(8,128)}, u32[]{:S(2)}) copy-start(f32[64,128]{1,0:T(8,128)} %param.11) | copy-start | bytes 98308
  89.8 6.0 %copy-start.4 = (f32[64,8]{0,1:T(8,128)S(1)}, f32[64,8]{0,1:T(8,128)}, u32[]{:S(2)}) copy-start(f32[64,8]{0,1:T(8,128)} %param.14) | copy-start | bytes 6148
  89.8 5.9 %copy-start = (bf16[64,32,256]{2,1,0:T(8,128)(2,1)}, bf16[64,32,256]{2,1,0:T(8,128)(2,1)S(1)}, u32[]{:S(2)}) copy-start(bf16[64,32,256]{2,1,0:T(8,128)(2,1)S(1)} %all-to-all-done.1) | copy-start | bytes 3145732
  89.9 54.2 %all-to-all-start = ((bf16[512,32,128]{2,1,0:T(8,128)(2,1)}), bf16[512,32,128]{2,1,0:T(8,128)(2,1)}, u32[]{:S(2)}, u32[]{:S(2)}) async-start(bf16[512,32,128]{2,1,0:T(8,128)(2,1)} %shard_map.82), calls=%async_computation | async-start | bytes 8388608 | tf_op jit(solution)/shard_map/all_to_all | solution.py:234
  95.1 44.1 %all-gather.3.cloned.1.call-start = ((), (), s32[]{:S(2)}) async-start(), calls=%async_computation.3 | async-start | bytes 1114112 | tf_op jit(solution)/shard_map/all_gather | solution.py:221
Sparse Core Ops, SparseCore 0:
  9.5 74.0 all-gather.4
  98.1 41.0 all-gather.2

commit v2 on v1

--- a/solution.py
+++ b/solution.py
@@ -58,7 +58,8 @@
     me, list_ref, count_ref, loc_ref, table_ref, prior_ref, obs_ref, state_ref, out_ref,
     seen, extra, system, diag, inv, qcol, *, nb, group, mode,
 ):
-    mems, entries, members_dev, width = obs_ref.shape
+    pieces, mems, entries, part, width = obs_ref.shape
+    members_dev = pieces * part
     members = mems * members_dev
     slots = list_ref.shape[1]
     regions = entries // slots
@@ -85,7 +86,9 @@
             both = table_ref[pl.ds(block, 1), :]
             live = jnp.where(l < count_ref[row], loc_ref[row, l], 0.0)
             scale = jnp.sqrt(live * both[:, :width])
-            picked = obs_ref[:, r * slots + l].reshape(members, width).astype(F32)
+            picked = jnp.concatenate(
+                [obs_ref[p, m, r * slots + l] for m in range(mems) for p in range(pieces)], axis=0
+            ).astype(F32)
             cols = slice(l * width, (l + 1) * width)
             seen[:, cols] = (picked * scale).astype(BF16)
             high, low = split(scale * both[:, width:])
@@ -186,15 +189,149 @@
     ]
 
 
-def collect(list_ref, all_ref, out_ref):
-    rows, slots = list_ref.shape
-
-    def one(r, carry):
-        for l in range(slots):
-            out_ref[r * slots + l] = all_ref[list_ref[r, l]]
-        return carry
-
-    lax.fori_loop(0, rows, one, 0)
+def exchange(
+    list_ref, own_ref, obs_ref, listed, send_sem, recv_sem, out_sem, in_sem, own_sem, *blocks, side
+):
+    pieces, count = own_ref.shape[:2]
+    mems, entries = obs_ref.shape[1:3]
+    slots = list_ref.shape[1]
+    half = count // 2
+    space, mem = lax.axis_index("space"), lax.axis_index("mem")
+    x, z = space // side, space % side
+
+    def at(axis, i, j):
+        dx, dz = (i, j) if axis == 0 else (j, i)
+        return (x + dx + side) % side * side + (z + dz + side) % side
+
+    barrier = pltpu.get_barrier_semaphore()
+    near = [at(0, 1, 0), at(0, -1, 0), at(0, 0, 1), at(0, 0, -1)]
+    for there in near:
+        pl.semaphore_signal(barrier, inc=1, device_id={"space": there, "mem": mem})
+    for step in range(1, mems):
+        pl.semaphore_signal(barrier, inc=1, device_id={"space": space, "mem": (mem + step) % mems})
+
+    own_copies = [
+        pltpu.make_async_copy(
+            own_ref.at[p], blocks[p].at[pl.ds(pl.multiple_of(space * count, count), count)], own_sem.at[p]
+        )
+        for p in range(pieces)
+    ]
+    for copy in own_copies:
+        copy.start()
+    pl.semaphore_wait(barrier, 4 + mems - 1)
+
+    def send(p, axis, number, chunk, part, to, own=False):
+        start, size = {"all": (0, half), "low": (0, half // 2), "high": (half // 2, half // 2)}[part]
+        start = start + axis * half
+        rows = pl.ds(pl.multiple_of(chunk * count + start, size), size)
+        src = own_ref.at[p, pl.ds(start, size)] if own else blocks[p].at[rows]
+        return pltpu.make_async_remote_copy(
+            src_ref=src,
+            dst_ref=blocks[p].at[rows],
+            send_sem=send_sem.at[p, axis, number],
+            recv_sem=recv_sem.at[p, axis, number],
+            device_id={"space": to, "mem": mem},
+        )
+
+    order = (0, -1, 1, 2)
+    sent = []
+
+    def copy_of(p, axis, number):
+        if number == 0:
+            return send(p, axis, 0, at(axis, 0, 0), "all", at(axis, 1, 0), True)
+        if number == 1:
+            return send(p, axis, 1, at(axis, 0, 0), "all", at(axis, -1, 0), True)
+        if number == 2:
+            return send(p, axis, 2, at(axis, -1, 0), "low", at(axis, 1, 0))
+        if number == 3:
+            return send(p, axis, 3, at(axis, 1, 0), "high", at(axis, -1, 0))
+        j, kind = (number - 4) // 4, (number - 4) % 4
+        d = order[j]
+        if kind == 0:
+            return send(p, axis, number, at(axis, d, 0), "all", at(axis, 0, 1), d == 0)
+        if kind == 1:
+            return send(p, axis, number, at(axis, d, 0), "all", at(axis, 0, -1), d == 0)
+        if kind == 2:
+            return send(p, axis, number, at(axis, d, -1), "low", at(axis, 0, 1))
+        return send(p, axis, number, at(axis, d, 1), "high", at(axis, 0, -1))
+
+    def start(p, *numbers):
+        for number in numbers:
+            for axis in (0, 1):
+                copy = copy_of(p, axis, number)
+                copy.start()
+                sent.append(copy)
+
+    def arrive(p, axis, *numbers):
+        for number in numbers:
+            copy_of(p, axis, number).wait_recv()
+
+    def begin(p):
+        start(p, 0, 1, 4, 5)
+
+    outgoing = []
+    begin(0)
+    for p in range(pieces):
+        for axis in (0, 1):
+            arrive(p, axis, 0)
+        start(p, 2, 8, 9)
+        for axis in (0, 1):
+            arrive(p, axis, 1)
+        start(p, 3, 12, 13)
+        for axis in (0, 1):
+            arrive(p, axis, 2, 3)
+        start(p, 16, 17)
+        if p + 1 < pieces:
+            begin(p + 1)
+        for j in range(4):
+            for kind in (0, 1):
+                for axis in (0, 1):
+                    arrive(p, axis, 4 + 4 * j + kind)
+                start(p, 4 + 4 * j + kind + 2)
+        for j in range(4):
+            for axis in (0, 1):
+                arrive(p, axis, 6 + 4 * j, 7 + 4 * j)
+        own_copies[p].wait()
+
+        def pick(r, carry, p=p):
+            for l in range(slots):
+                listed[p, r * slots + l] = blocks[p][list_ref[r, l]]
+            return carry
+
+        lax.fori_loop(0, list_ref.shape[0], pick, 0)
+        mine = pltpu.make_async_copy(
+            listed.at[p, pl.ds(pl.multiple_of(mem * entries, entries), entries)],
+            obs_ref.at[p, mem],
+            own_sem.at[pieces + p],
+        )
+        mine.start()
+        own_copies.append(mine)
+        for step in range(1, mems):
+            to = (mem + step) % mems
+            copy = pltpu.make_async_remote_copy(
+                src_ref=listed.at[p, pl.ds(pl.multiple_of(to * entries, entries), entries)],
+                dst_ref=obs_ref.at[p, mem],
+                send_sem=out_sem.at[p, step],
+                recv_sem=in_sem.at[p, step],
+                device_id={"space": space, "mem": to},
+            )
+            copy.start()
+            outgoing.append((p, step, copy))
+
+    for p in range(pieces):
+        own_copies[pieces + p].wait()
+    for p, step, copy in outgoing:
+        source = (mem - step + mems) % mems
+        pltpu.make_async_remote_copy(
+            src_ref=listed.at[p, pl.ds(0, entries)],
+            dst_ref=obs_ref.at[p, source],
+            send_sem=out_sem.at[p, step],
+            recv_sem=in_sem.at[p, step],
+            device_id={"space": space, "mem": source},
+        ).wait_recv()
+        copy.wait_send()
+    for copy in sent:
+        copy.wait_send()
 
 
 def analyse_here(*refs, nb, group, mode):
@@ -208,31 +345,41 @@
 def body(
     ensemble_state, obs_ens, innovation, obs_prec, block_list, block_count, loc_weight, prior_weight
 ):
-    mems = lax.axis_size("mem")
+    spaces, mems = lax.axis_size("space"), lax.axis_size("mem")
     members_dev, regions_dev, p_size = ensemble_state.shape
-    width = obs_ens.shape[2]
+    blocks_dev, width = obs_ens.shape[1:]
     slots = block_list.shape[1]
     regions = regions_dev // mems
     entries = regions * slots
     members = members_dev * mems
-    params = pltpu.CompilerParams(vmem_limit_bytes=56 << 20)
+    pieces = 2
+    part = members_dev // pieces
+    dma = pltpu.SemaphoreType.DMA
 
     table = jnp.concatenate([obs_prec, innovation], axis=1)
     table = lax.all_gather(table, "space", axis=0, tiled=True)
-    blocks = jnp.transpose(obs_ens, (1, 0, 2))
-    blocks = lax.all_gather(blocks, "space", axis=0, tiled=True)
     states = jnp.transpose(ensemble_state, (1, 0, 2))
     states = lax.all_to_all(states, "mem", split_axis=0, concat_axis=0, tiled=True)
     states = states.reshape(mems, regions, members_dev, p_size)
-    listed = pl.pallas_call(
-        collect,
+    own = jnp.transpose(obs_ens.reshape(pieces, part, blocks_dev, width), (0, 2, 1, 3))
+    seen = pl.pallas_call(
+        functools.partial(exchange, side=math.isqrt(spaces)),
         in_specs=[SMEM, VMEM],
         out_specs=VMEM,
-        out_shape=jax.ShapeDtypeStruct((regions_dev * slots, members_dev, width), BF16),
-        compiler_params=params,
-    )(block_list, blocks)
-    seen = lax.all_to_all(listed, "mem", split_axis=0, concat_axis=0, tiled=True)
-    seen = seen.reshape(mems, entries, members_dev, width)
+        out_shape=jax.ShapeDtypeStruct((pieces, mems, entries, part, width), BF16),
+        scratch_shapes=[
+            pltpu.VMEM((pieces, regions_dev * slots, part, width), BF16),
+            dma((pieces, 2, 20)),
+            dma((pieces, 2, 20)),
+            dma((pieces, mems)),
+            dma((pieces, mems)),
+            dma((2 * pieces,)),
+            *[pltpu.VMEM((blocks_dev * spaces, part, width), BF16) for _ in range(pieces)],
+        ],
+        compiler_params=pltpu.CompilerParams(
+            vmem_limit_bytes=48 << 20, collective_id=0, has_side_effects=True
+        ),
+    )(block_list, own)
     nb = 64
     updated = pl.pallas_call(
         functools.partial(analyse_here, nb=nb, group=8, mode=6),
@@ -240,7 +387,7 @@
         out_specs=VMEM,
         out_shape=jax.ShapeDtypeStruct((mems, regions, members_dev, p_size), BF16),
         scratch_shapes=analysis_scratch(members, regions, slots, width, nb),
-        compiler_params=params,
+        compiler_params=pltpu.CompilerParams(vmem_limit_bytes=48 << 20),
     )(block_list, block_count, loc_weight, table, prior_weight, seen, states)
     updated = updated.reshape(regions_dev, members_dev, p_size)
     updated = lax.all_to_all(updated, "mem", split_axis=0, concat_axis=0, tiled=True)

time: 223 us -> 188 us (0.84)
  waiting for transfers between devices: 113 us -> 0.02 us
  Pallas kernels: 57.1 us -> 141 us
  starting transfers between devices: 11.2 us -> 6.1 us
    pallas_call x1, Pallas kernels: 6.23 us -> 91.6 us  [body(): pl.pallas_call(functools.partial(exchange, side=math.isqrt(spaces)), in_s...]
    all_gather x1 -> x0, waiting for transfers between devices: 65.4 us -> none  [body(): blocks = lax.all_gather(blocks, 'space', axis=0, tiled=True)]
    all_gather x1, waiting for transfers between devices: 42.7 us -> 0.01 us  [body(): table = lax.all_gather(table, 'space', axis=0, tiled=True)]
    all_to_all x1 -> x0, starting transfers between devices: 5.24 us -> none  [body(): lax.all_to_all(listed, 'mem', split_axis=0, concat_axis=0, tiled=True)]
    all_to_all x1 -> x0, waiting for transfers between devices: 4.81 us -> none  [body(): lax.all_to_all(listed, 'mem', split_axis=0, concat_axis=0, tiled=True)]
    unnamed x14 -> x17, local copies, waits for them, and re-layouts: 6.4 us -> 6.13 us
  transfers between devices with their start and end apart: 4 -> 2, of which waited for: 3 -> 0; matrix products, arithmetic and copies ran while one was open for 2% -> 2% of each run, Pallas kernels for 3% -> 49%
where the time goes in v2:
time: 188 us; the launch traced here: 187 us
  Pallas kernels  141 us (75%)
  blocking collectives  17.5 us (9%)
  between operations  13.4 us (7%)
  local copies, waits for them, and re-layouts  8.03 us (4%)
  starting transfers between devices  6.1 us (3%)
    pallas_call x1, Pallas kernels, body(): pl.pallas_call(functools.partial(exchange, side=math.isqrt(spaces)), in_s...  91.6 us
    pallas_call x1, Pallas kernels, body(): pl.pallas_call(functools.partial(analyse_here, nb=nb, group=8, mode=6), i...  49.2 us
    all_to_all x1, blocking collectives, body(): lax.all_to_all(updated, 'mem', split_axis=0, concat_axis=0, tiled=True)  17.5 us
    unnamed x17, local copies, waits for them, and re-layouts  6.13 us
    all_to_all x1, starting transfers between devices, body(): lax.all_to_all(states, 'mem', split_axis=0, concat_axis=0, tiled=True)  6.1 us
  transfers between devices with their start and end apart: 2, of which 0 were waited for; matrix products, arithmetic and copies ran while one was open for 2% of the time, Pallas kernels for 49%

profile of v2, /device:TPU:1, one launch (start us, length us, event | category | flops | bytes accessed | tf_op | source)
XLA Modules:
  0.0 187.3 jit_solution(2644458248940067347)
XLA Ops:
  6.5 0.0 copy-start.5
  6.5 0.0 copy-start.6
  6.5 0.0 copy-start.4
  6.5 0.0 all-gather.2.cloned.1.call-start
  6.5 1.5 pad_maximum_fusion
  8.0 0.0 all-gather.2.cloned.1.call-update
  8.0 2.8 %copy.28 = bf16[32,64,256]{2,0,1:T(8,128)(2,1)} copy(bf16[32,64,256]{2,1,0:T(8,128)(2,1)} %param.8) | data formatting | bytes 2097152 | tf_op args[0]
  10.8 0.0 copy-start.2
  10.8 0.0 copy-start.3
  10.8 6.1 %all-to-all-start = ((bf16[64,32,256]{2,1,0:T(8,128)(2,1)}), bf16[64,32,256]{2,1,0:T(8,128)(2,1)S(1)}, u32[]{:S(2)}, u32[]{:S(2)}) async-start(bf16[64,32,256]{2,1,0:T(8,128)(2,1)} %bitcast.8), calls=%async_computation | async-start | bytes 2097152 | tf_op jit(solution)/shard_map/all_to_all | solution.py:362
  16.9 0.0 copy-done.5
  16.9 0.1 copy.23.list_ref.refs_0_
  17.0 0.0 copy-done.6
  17.0 0.1 copy.24.refs_2_
  17.1 0.0 copy-done.4
  17.1 0.3 copy.29
  17.4 91.6 %shard_map.82.refs_5_ = bf16[2,8,64,16,128]{4,3,2,1,0:T(8,128)(2,1)S(1)} custom-call(s32[64,8]{1,0:T(8,128)S(1)} %copy.23.list_ref.refs_0_, bf16[2,64,16,128]{3,2,1,0:T(8,128)(2,1)S(1)} %bitcast.12), custom_call_target="tpu_custom_call" | custom-call | tf_op jit(solution)/shard_map/pallas_call | solution.py:365
  109.0 0.0 copy-start
  109.0 1.9 %copy-done = bf16[2,8,64,16,128]{4,3,2,1,0:T(8,128)(2,1)} copy-done((bf16[2,8,64,16,128]{4,3,2,1,0:T(8,128)(2,1)}, bf16[2,8,64,16,128]{4,3,2,1,0:T(8,128)(2,1)S(1)}, u32[]{:S(2)}) %copy-start) | copy-done | bytes 4194328
  111.0 0.0 all-to-all-done
  111.0 0.0 all-gather.2.cloned.1.call-done.refs_3_
  111.0 0.0 copy-done.2
  111.0 0.0 copy-done.3
  111.0 0.0 copy-start.1
  111.0 1.2 copy-done.1
  112.2 49.2 %shard_map.83 = bf16[8,8,32,256]{3,2,1,0:T(8,128)(2,1)S(1)} custom-call(s32[64,8]{1,0:T(8,128)S(1)} %copy.23.list_ref.refs_0_, s32[64]{0:T(128)S(1)} %copy-done.3, f32[64,8]{1,0:T(8,128)S(1)} %copy.24.refs_2_, f32[1024,256]{1,0:T(8,128)S(1)} %copy-done.1, f32[64,256]{1,0:T(8,128)S(1)} %copy-done.2, bf16[2,8,64,16,128]{4,3,2,1,0:T(8,128)(2,1)} %copy-done, ...), custom_call_target="tpu_custom_call" | custom-call | tf_op jit(solution)/shard_map/pallas_call | solution.py:384
  161.4 17.5 %all_to_all.10 = bf16[64,32,256]{2,1,0:T(8,128)(2,1)S(1)} all-to-all(bf16[64,32,256]{2,1,0:T(8,128)(2,1)S(1)} %bitcast.11), channel_id=1, replica_groups=mesh['space'=16,'mem'=8] {'mem'}, dimensions={0} | all-to-all | bytes 2097152 | tf_op jit(solution)/shard_map/all_to_all | solution.py:393
  178.9 1.6 copy.25
Async XLA Ops:
  6.5 10.4 %copy-start.5 = (s32[64,8]{0,1:T(8,128)S(1)}, s32[64,8]{0,1:T(8,128)}, u32[]{:S(2)}) copy-start(s32[64,8]{0,1:T(8,128)} %param.12) | copy-start | bytes 6148
  6.5 10.5 %copy-start.6 = (f32[64,8]{0,1:T(8,128)S(1)}, f32[64,8]{0,1:T(8,128)}, u32[]{:S(2)}) copy-start(f32[64,8]{0,1:T(8,128)} %param.14) | copy-start | bytes 6148
  6.5 10.5 %copy-start.4 = (bf16[32,64,128]{2,1,0:T(8,128)(2,1)S(1)}, bf16[32,64,128]{2,1,0:T(8,128)(2,1)}, u32[]{:S(2)}) copy-start(bf16[32,64,128]{2,1,0:T(8,128)(2,1)} %param.9) | copy-start | bytes 1572868
  6.5 104.4 %all-gather.2.cloned.1.call-start = ((), (), s32[]{:S(2)}) async-start(), calls=%async_computation.2 | async-start | bytes 1114112 | tf_op jit(solution)/shard_map/all_gather | solution.py:360
  10.8 100.2 %copy-start.2 = (f32[64,256]{1,0:T(8,128)S(1)}, f32[64,256]{1,0:T(8,128)}, u32[]{:S(2)}) copy-start(f32[64,256]{1,0:T(8,128)} %refs_4_.1) | copy-start | bytes 196612
  10.8 100.2 %copy-start.3 = (s32[64]{0:T(128)S(1)}, s32[64]{0:T(128)}, u32[]{:S(2)}) copy-start(s32[64]{0:T(128)} %refs_1_.1) | copy-start | bytes 772
  10.8 100.2 %all-to-all-start = ((bf16[64,32,256]{2,1,0:T(8,128)(2,1)}), bf16[64,32,256]{2,1,0:T(8,128)(2,1)S(1)}, u32[]{:S(2)}, u32[]{:S(2)}) async-start(bf16[64,32,256]{2,1,0:T(8,128)(2,1)} %bitcast.8), calls=%async_computation | async-start | bytes 2097152 | tf_op jit(solution)/shard_map/all_to_all | solution.py:362
  109.0 2.0 %copy-start = (bf16[2,8,64,16,128]{4,3,2,1,0:T(8,128)(2,1)}, bf16[2,8,64,16,128]{4,3,2,1,0:T(8,128)(2,1)S(1)}, u32[]{:S(2)}) copy-start(bf16[2,8,64,16,128]{4,3,2,1,0:T(8,128)(2,1)S(1)} %shard_map.82.refs_5_) | copy-start | bytes 12582916
  111.0 1.2 copy-start.1
Sparse Core Ops, SparseCore 0:
  9.5 48.0 all-gather.1

commit v3 on v1

v3 whole, which is shorter than its diff:
```python
import functools
import math

import jax
import jax.numpy as jnp
from jax import lax
from jax.experimental import pallas as pl
from jax.experimental.pallas import tpu as pltpu
from jax.sharding import PartitionSpec as P

INFLATION = 1.1
HIGHEST = lax.Precision.HIGHEST
F32 = jnp.float32
BF16 = jnp.bfloat16


def dot(a, b, dims, precision=None):
    return lax.dot_general(a, b, (dims, ((), ())), precision=precision, preferred_element_type=F32)


def split(x):
    high = x.astype(BF16)
    return high, (x - high.astype(F32)).astype(BF16)


def eliminate(rows, group):
    count = len(rows)
    rows = list(rows)

    def lane(x, i):
        return jnp.broadcast_to(x[:, i : i + 1], x.shape)

    for k in range(0, count, group):
        small = {(a, b): lane(rows[k + a], k + b) for a in range(group) for b in range(a, group)}
        for a in range(group):
            root = lax.rsqrt(small[a, a])
            upper = {b: small[a, b] * root for b in range(a + 1, group)}
            rows[k + a] = rows[k + a] * root
            for c in range(a + 1, group):
                rows[k + c] = rows[k + c] - upper[c] * rows[k + a]
                for b in range(c, group):
                    small[c, b] = small[c, b] - upper[c] * upper[b]
        for i in range(k + group, count):
            for a in range(group):
                rows[i] = rows[i] - lane(rows[k + a], i) * rows[k + a]
    return rows


def whole(
    list_ref, count_ref, loc_ref, state_ref, obs_ref, prec_ref, innov_ref, prior_ref,
    out_ref,
    listed, seen_obs, table, states_in, wide, result, seen, extra, system, diag, vectors, qcol,
    ring_send, ring_recv, obs_send, obs_recv, state_send, state_recv, out_send, out_recv, own_sem,
    table_send, table_recv,
    *blocks, side, nb, group,
):
    pieces, mems, entries, part, width = seen_obs.shape
    members_dev, count = obs_ref.shape[:2]
    rows_space, slots = list_ref.shape
    regions = rows_space // mems
    members = mems * members_dev
    p_size = state_ref.shape[2]
    half = count // 2
    space, mem = lax.axis_index("space"), lax.axis_index("mem")
    core = mem % 2
    x, z = space // side, space % side
    first = mem * regions

    def at(axis, i, j):
        dx, dz = (i, j) if axis == 0 else (j, i)
        return (x + dx + side) % side * side + (z + dz + side) % side

    def peer(step):
        return (mem + step) % mems

    barrier = pltpu.get_barrier_semaphore()
    for there in [at(0, 1, 0), at(0, -1, 0), at(0, 0, 1), at(0, 0, -1)]:
        pl.semaphore_signal(barrier, inc=1, device_id={"space": there, "mem": mem})
    for step in range(1, mems):
        pl.semaphore_signal(barrier, inc=1, device_id={"space": space, "mem": peer(step)})

    for k in range(members_dev):
        wide[0, k * count : (k + 1) * count, :] = obs_ref[k].astype(F32)

    def turn(b, carry):
        block = wide[0, pl.ds(b, members_dev, stride=count), :].astype(BF16)
        for p in range(pieces):
            blocks[p][space * count + b] = block[p * part : (p + 1) * part]
        return carry

    lax.fori_loop(0, count, turn, 0, unroll=4)
    here = pl.ds(pl.multiple_of(space * count, count), count)
    table[core, here, :] = jnp.where(core == 0, prec_ref[...], innov_ref[...])
    pl.semaphore_wait(barrier, 4 + mems - 1)

    rings = [*blocks, table.at[core]]

    def send(p, axis, number, chunk, share, to):
        start, size = {"all": (0, half), "low": (0, half // 2), "high": (half // 2, half // 2)}[share]
        rows = pl.ds(pl.multiple_of(chunk * count + start + axis * half, size), size)
        return pltpu.make_async_remote_copy(
            src_ref=rings[p].at[rows],
            dst_ref=rings[p].at[rows],
            send_sem=ring_send.at[p, axis, number],
            recv_sem=ring_recv.at[p, axis, number],
            device_id={"space": to, "mem": mem},
        )

    order = (0, -1, 1, 2)

    def copy_of(p, axis, number):
        if number == 0:
            return send(p, axis, 0, at(axis, 0, 0), "all", at(axis, 1, 0))
        if number == 1:
            return send(p, axis, 1, at(axis, 0, 0), "all", at(axis, -1, 0))
        if number == 2:
            return send(p, axis, 2, at(axis, -1, 0), "low", at(axis, 1, 0))
        if number == 3:
            return send(p, axis, 3, at(axis, 1, 0), "high", at(axis, -1, 0))
        d, kind = order[(number - 4) // 4], (number - 4) % 4
        if kind == 0:
            return send(p, axis, number, at(axis, d, 0), "all", at(axis, 0, 1))
        if kind == 1:
            return send(p, axis, number, at(axis, d, 0), "all", at(axis, 0, -1))
        if kind == 2:
            return send(p, axis, number, at(axis, d, -1), "low", at(axis, 0, 1))
        return send(p, axis, number, at(axis, d, 1), "high", at(axis, 0, -1))

    sent = []

    def start(p, *numbers):
        for number in numbers:
            for axis in (0, 1):
                copy = copy_of(p, axis, number)
                copy.start()
                sent.append(copy)

    def arrive(p, *numbers):
        for number in numbers:
            for axis in (0, 1):
                copy_of(p, axis, number).wait_recv()

    def begin(p):
        start(p, 0, 1, 4, 5)

    def state_copy(step):
        to = peer(step)
        return pltpu.make_async_remote_copy(
            src_ref=state_ref.at[:, pl.ds(pl.multiple_of(to * regions, regions), regions), :],
            dst_ref=states_in.at[mem],
            send_sem=state_send.at[step],
            recv_sem=state_recv.at[step],
            device_id={"space": space, "mem": to},
        )

    def obs_copy(p, step):
        to = peer(step)
        return pltpu.make_async_remote_copy(
            src_ref=listed.at[p, pl.ds(pl.multiple_of(to * entries, entries), entries)],
            dst_ref=seen_obs.at[p, mem],
            send_sem=obs_send.at[p, step],
            recv_sem=obs_recv.at[p, step],
            device_id={"space": space, "mem": to},
        )

    local = []

    def begin_states():
        copy = pltpu.make_async_copy(
            state_ref.at[:, pl.ds(pl.multiple_of(first, regions), regions), :],
            states_in.at[mem],
            own_sem.at[pieces],
        )
        copy.start()
        local.append(copy)
        for step in range(1, mems):
            state_copy(step).start()

    sequence = [0, pieces, *range(1, pieces)]
    begin(0)
    begin_states()
    for turn_number, p in enumerate(sequence):
        arrive(p, 0)
        start(p, 2, 8, 9)
        arrive(p, 1)
        start(p, 3, 12, 13)
        arrive(p, 2, 3)
        start(p, 16, 17)
        if turn_number + 1 < len(sequence):
            begin(sequence[turn_number + 1])
        for j in range(4):
            for kind in (0, 1):
                arrive(p, 4 + 4 * j + kind)
                start(p, 4 + 4 * j + kind + 2)
        for j in range(4):
            arrive(p, 6 + 4 * j, 7 + 4 * j)
        if p == pieces:
            other = pltpu.make_async_remote_copy(
                src_ref=table.at[core],
                dst_ref=table.at[core],
                send_sem=table_send,
                recv_sem=table_recv,
                device_id={"space": space, "mem": mem + 1 - 2 * core},
            )
            other.start()
            continue

        def pick(r, carry, p=p):
            for l in range(slots):
                listed[p, r * slots + l] = blocks[p][list_ref[r, l]]
            return carry

        lax.fori_loop(0, rows_space, pick, 0)
        mine = pltpu.make_async_copy(
            listed.at[p, pl.ds(pl.multiple_of(mem * entries, entries), entries)],
            seen_obs.at[p, mem],
            own_sem.at[p],
        )
        mine.start()
        local.append(mine)
        for step in range(1, mems):
            obs_copy(p, step).start()

    extra[...] = jnp.zeros_like(extra)
    shares_all = prior_ref[pl.ds(pl.multiple_of(first, regions), regions), :]
    shares_all = shares_all / jnp.sum(shares_all, axis=1, keepdims=True)
    root_t = jnp.transpose(jnp.sqrt(members * shares_all))
    for r in range(regions):
        qcol[r] = jnp.broadcast_to(root_t[:, r : r + 1], (members, 128))
    halves = members // 128
    for step in range(1, mems):
        state_copy(step).wait_recv()
    local[0].wait()
    for m in range(mems):
        many = states_in[m].astype(F32).reshape(members_dev * regions, p_size)
        for h in range(p_size // 128):
            wide[h, m * members_dev * regions : (m + 1) * members_dev * regions, :] = many[
                :, h * 128 : (h + 1) * 128
            ]
    other.wait()
    for copy in sent:
        copy.wait_send()
    for step in range(1, mems):
        state_copy(step).wait_send()
    for copy in local[1:]:
        copy.wait()
    for p in range(pieces):
        for step in range(1, mems):
            obs_copy(p, step).wait()

    row_id = lax.broadcasted_iota(jnp.int32, (members, members), 0)
    col_id = lax.broadcasted_iota(jnp.int32, (members, members), 1)

    def shares_of(r):
        s = prior_ref[pl.ds(first + r, 1), :]
        return s / jnp.sum(s, axis=1, keepdims=True)

    def build(r, carry):
        row = first + r
        for l in range(slots):
            block = list_ref[row, l]
            live = jnp.where(l < count_ref[row], loc_ref[row, l], 0.0)
            scale = jnp.sqrt(live * table[0, pl.ds(block, 1), :])
            picked = jnp.concatenate(
                [seen_obs[p, m, r * slots + l] for m in range(mems) for p in range(pieces)], axis=0
            ).astype(F32)
            cols = slice(l * width, (l + 1) * width)
            seen[:, cols] = (picked * scale).astype(BF16)
            high, low = split(scale * table[1, pl.ds(block, 1), :])
            extra[0:1, cols] = high.astype(F32)
            extra[1:2, cols] = low.astype(F32)
        all_seen = seen[...]
        gram = dot(all_seen, all_seen, ((1,), (1,)))
        proj = dot(extra[...].astype(BF16), all_seen, ((1,), (1,)))
        proj = proj[0:1] + proj[1:2]
        shares = shares_of(r)
        root = jnp.sqrt(members * shares)
        left = dot(jnp.broadcast_to(shares, (8, members)), gram, ((1,), (0,)), HIGHEST)[0:1]
        centred = gram - left
        centred = centred - jnp.sum(centred * shares, axis=1, keepdims=True)
        q = jnp.concatenate([qcol[r]] * halves, axis=1)
        full = q * centred * root + jnp.where(row_id == col_id, (members - 1) / INFLATION, 0.0)
        at_r = pl.ds(pl.multiple_of(r * members, members), members)
        for h in range(halves):
            system[h, at_r, :] = full[:, h * 128 : (h + 1) * 128]
        vectors[pl.ds(r, 1), :] = root * (proj - jnp.sum(shares * proj, axis=1, keepdims=True))
        return carry

    lax.fori_loop(0, regions, build, 0, unroll=2)

    lane_id = lax.broadcasted_iota(jnp.int32, (regions, 128), 1)
    for b in range(members // nb):
        h_b, place = b * nb // 128, b * nb % 128
        rows = []
        for i in range(nb):
            row = system[h_b, pl.ds(b * nb + i, regions, stride=members), :]
            if place:
                row = pltpu.roll(row, 128 - place, 1)
            rows.append(jnp.where(lane_id < nb, row, jnp.where(lane_id == nb + i, 1.0, 0.0)))
        rows = eliminate(rows, group)
        for i in range(nb):
            diag[pl.ds(i, regions, stride=nb), :] = rows[i]

        def sweep(r, carry, b=b, h_b=h_b, place=place):
            begins = r * members + b * nb
            band_rows = pl.ds(pl.multiple_of(begins, nb), nb)
            small = diag[pl.ds(pl.multiple_of(r * nb, nb), nb), :][:, nb : 2 * nb]
            band = jnp.concatenate([system[h, band_rows, :] for h in range(halves)], axis=1)
            ids = lax.broadcasted_iota(jnp.int32, (nb, members), 1)
            rid = lax.broadcasted_iota(jnp.int32, (nb, members), 0)
            mine = (ids >= b * nb) & (ids < (b + 1) * nb)
            band = jnp.where(mine, jnp.where(ids - b * nb == rid, 1.0, 0.0), band)
            done = dot(small, band, ((1,), (0,)), HIGHEST)
            kept = jnp.where(ids < (b + 1) * nb, done, 0.0)
            for h in range(halves):
                system[h, band_rows, :] = kept[:, h * 128 : (h + 1) * 128]
            rest = members - (b + 1) * nb
            if rest:
                below = pl.ds(pl.multiple_of(begins + nb, nb), rest)
                change = dot(done[:, (b + 1) * nb :], done, ((0,), (0,)), HIGHEST)
                for h in range(halves):
                    old = system[h, below, :]
                    if h == h_b:
                        lanes = lax.broadcasted_iota(jnp.int32, (rest, 128), 1)
                        old = jnp.where((lanes >= place) & (lanes < place + nb), 0.0, old)
                    system[h, below, :] = old - change[:, h * 128 : (h + 1) * 128]
            return carry

        lax.fori_loop(0, regions, sweep, 0, unroll=True)

    def out_copy(r, step):
        to = peer(step)
        return pltpu.make_async_remote_copy(
            src_ref=result.at[r, pl.ds(pl.multiple_of(to * members_dev, members_dev), members_dev), :],
            dst_ref=out_ref.at[first + r],
            send_sem=out_send.at[r, step],
            recv_sem=out_recv.at[r, step],
            device_id={"space": space, "mem": to},
        )

    def own_out(r):
        return pltpu.make_async_copy(
            result.at[r, pl.ds(pl.multiple_of(mem * members_dev, members_dev), members_dev), :],
            out_ref.at[first + r],
            out_send.at[r, 0],
        )

    def finish(r, carry):
        at_r = pl.ds(pl.multiple_of(r * members, members), members)
        inverse = jnp.concatenate([system[h, at_r, :] for h in range(halves)], axis=1)
        shares = shares_of(r)
        root = jnp.sqrt(members * shares)
        solved = jnp.sum(inverse * vectors[pl.ds(r, 1), :], axis=1, keepdims=True)
        weights = jnp.sum(inverse * solved, axis=0, keepdims=True)
        mixing = root * (weights + math.sqrt(members - 1.0) * inverse)
        mixing = mixing - jnp.sum(mixing, axis=1, keepdims=True) * shares + shares
        high, low = split(mixing)
        states = jnp.concatenate(
            [wide[h, pl.ds(r, members, stride=regions), :] for h in range(p_size // 128)], axis=1
        ).astype(BF16)
        done = dot(high, states, ((1,), (0,))) + dot(low, states, ((1,), (0,)))
        result[r] = done.astype(BF16)
        own_out(r).start()
        for step in range(1, mems):
            out_copy(r, step).start()
        return carry

    lax.fori_loop(0, regions, finish, 0)

    def close(r, carry):
        own_out(r).wait()
        for step in range(1, mems):
            out_copy(r, step).wait()
        return carry

    lax.fori_loop(0, regions, close, 0)


SMEM = pl.BlockSpec(memory_space=pltpu.SMEM)
VMEM = pl.BlockSpec(memory_space=pltpu.VMEM)
ANY = pl.BlockSpec(memory_space=pl.ANY)


def body(
    ensemble_state, obs_ens, innovation, obs_prec, block_list, block_count, loc_weight, prior_weight
):
    spaces, mems = lax.axis_size("space"), lax.axis_size("mem")
    members_dev, regions_dev, p_size = ensemble_state.shape
    blocks_dev, width = obs_ens.shape[1:]
    slots = block_list.shape[1]
    regions = regions_dev // mems
    entries = regions * slots
    members = members_dev * mems
    pieces = 4
    part = members_dev // pieces
    nb = 64
    dma = pltpu.SemaphoreType.DMA
    updated = pl.pallas_call(
        functools.partial(whole, side=math.isqrt(spaces), nb=nb, group=8),
        in_specs=[SMEM, SMEM, SMEM, ANY, VMEM, VMEM, VMEM, VMEM],
        out_specs=VMEM,
        out_shape=jax.ShapeDtypeStruct((regions_dev, members_dev, p_size), BF16),
        scratch_shapes=[
            pltpu.VMEM((pieces, regions_dev * slots, part, width), BF16),
            pltpu.VMEM((pieces, mems, entries, part, width), BF16),
            pltpu.VMEM((2, blocks_dev * spaces, width), F32),
            pltpu.VMEM((mems, members_dev, regions, p_size), BF16),
            pltpu.VMEM((p_size // 128, max(members * regions, members_dev * blocks_dev), 128), F32),
            pltpu.VMEM((regions, members, p_size), BF16),
            pltpu.VMEM((members, slots * width), BF16),
            pltpu.VMEM((16, slots * width), F32),
            pltpu.VMEM((members // 128, regions * members, 128), F32),
            pltpu.VMEM((regions * nb, 128), F32),
            pltpu.VMEM((regions, members), F32),
            pltpu.VMEM((regions, members, 128), F32),
            dma((pieces + 1, 2, 20)),
            dma((pieces + 1, 2, 20)),
            dma((pieces, mems)),
            dma((pieces, mems)),
            dma((mems,)),
            dma((mems,)),
            dma((regions, mems)),
            dma((regions, mems)),
            dma((pieces + 1,)),
            dma(()),
            dma(()),
            *[pltpu.VMEM((blocks_dev * spaces, part, width), BF16) for _ in range(pieces)],
        ],
        compiler_params=pltpu.CompilerParams(
            vmem_limit_bytes=52 << 20, collective_id=0, has_side_effects=True
        ),
    )(block_list, block_count, loc_weight, ensemble_state, obs_ens, obs_prec, innovation, prior_weight)
    return jnp.transpose(updated, (1, 0, 2))


def solution(mesh):
    return jax.shard_map(
        body,
        mesh=mesh,
        in_specs=(
            P("mem", "space", None),
            P("mem", "space", None),
            P("space", None),
            P("space", None),
            P("space", None),
            P("space"),
            P("space", None),
            P("space", None),
        ),
        out_specs=P("mem", "space", None),
        check_vma=False,
    )
```

time: 223 us -> 142 us (0.64)
  waiting for transfers between devices: 113 us -> 0 us
  Pallas kernels: 57.1 us -> 136 us
  blocking collectives: 19.4 us -> 0 us
  between operations: 13.4 us -> 0.03 us
  starting transfers between devices: 11.2 us -> 0 us
  local copies, waits for them, and re-layouts: 7.96 us -> 5.7 us
    all_gather x2 -> x0, waiting for transfers between devices: 108 us -> none  [the longest x1 65.4 us: body(): blocks = lax.all_gather(blocks, 'space', axis=0, tiled=True)]
    pallas_call x2 -> x1, Pallas kernels: 57.1 us -> 136 us  [body(): pl.pallas_call(functools.partial(whole, side=math.isqrt(spaces), nb=nb, g...]
    all_to_all x1 -> x0, blocking collectives: 19.4 us -> none  [body(): lax.all_to_all(updated, 'mem', split_axis=0, concat_axis=0, tiled=True)]
    all_to_all x2 -> x0, starting transfers between devices: 11.2 us -> none  [the longest x1 5.97 us: body(): lax.all_to_all(states, 'mem', split_axis=0, concat_axis=0, tiled=True)]
    all_to_all x2 -> x0, waiting for transfers between devices: 4.82 us -> none  [the longest x1 4.81 us: body(): lax.all_to_all(listed, 'mem', split_axis=0, concat_axis=0, tiled=True)]
    unnamed x14 -> x12, local copies, waits for them, and re-layouts: 6.4 us -> 4.14 us
  transfers between devices with their start and end apart: 4 -> 0, of which waited for: 3 -> 0; matrix products, arithmetic and copies ran while one was open for 2% -> 0% of each run, Pallas kernels for 3% -> 0%
where the time goes in v3:
time: 142 us
  Pallas kernels  136 us (96%)
  local copies, waits for them, and re-layouts  5.7 us (4%)
    pallas_call x1, Pallas kernels, body(): pl.pallas_call(functools.partial(whole, side=math.isqrt(spaces), nb=nb, g...  136 us
    unnamed x12, local copies, waits for them, and re-layouts  4.14 us

profile of v3, /device:TPU:1, one launch (start us, length us, event | category | flops | bytes accessed | tf_op | source)
XLA Modules:
  0.0 141.5 jit_solution(17944663530701905660)
XLA Ops:
  0.0 0.0 copy-start.1
  0.0 0.8 copy.9.list_ref
  0.8 0.0 copy-start.4
  0.8 0.8 copy.10.loc_ref
  1.6 0.0 copy-done.1
  1.6 0.0 copy-done.4
  1.6 0.0 copy-start
  1.6 1.0 copy-done
  2.6 0.0 copy-start.2
  2.6 0.8 copy-done.2
  3.4 0.0 copy-start.3
  3.4 0.8 copy-done.3
  4.2 135.8 %shard_map.82 = bf16[64,32,256]{2,1,0:T(8,128)(2,1)S(1)} custom-call(s32[64,8]{1,0:T(8,128)S(1)} %copy.9.list_ref, s32[64]{0:T(128)S(1)} %copy-done.4, f32[64,8]{1,0:T(8,128)S(1)} %copy.10.loc_ref, bf16[32,64,256]{2,1,0:T(8,128)(2,1)} %state_ref.1, bf16[32,64,128]{2,1,0:T(8,128)(2,1)S(1)} %copy-done, f32[64,128]{1,0:T(8,128)S(1)} %copy-done.2, ...), custom_call_target="tpu_custom_call" | custom-call | tf_op jit(solution)/shard_map/pallas_call | solution.py:398
  140.0 1.6 %copy.11 = bf16[32,64,256]{2,1,0:T(8,128)(2,1)} copy(bf16[32,64,256]{2,0,1:T(8,128)(2,1)S(1)} %bitcast.1) | data formatting | bytes 2097152 | tf_op jit(solution)/shard_map/transpose | solution.py:433
Async XLA Ops:
  0.0 1.6 %copy-start.1 = (f32[64,256]{1,0:T(8,128)S(1)}, f32[64,256]{1,0:T(8,128)}, u32[]{:S(2)}) copy-start(f32[64,256]{1,0:T(8,128)} %prior_ref.1) | copy-start | bytes 196612
  0.8 0.8 copy-start.4
  1.6 1.0 copy-start
  2.6 0.8 copy-start.2
  3.4 0.8 copy-start.3

commit v4 on v3

--- a/solution.py
+++ b/solution.py
@@ -23,12 +23,12 @@
     return high, (x - high.astype(F32)).astype(BF16)
 
 
-def eliminate(rows, group):
+def eliminate(rows, group, first):
     count = len(rows)
     rows = list(rows)
 
     def lane(x, i):
-        return jnp.broadcast_to(x[:, i : i + 1], x.shape)
+        return jnp.broadcast_to(x[:, first + i : first + i + 1], x.shape)
 
     for k in range(0, count, group):
         small = {(a, b): lane(rows[k + a], k + b) for a in range(group) for b in range(a, group)}
@@ -47,16 +47,16 @@
 
 
 def whole(
-    list_ref, count_ref, loc_ref, state_ref, obs_ref, prec_ref, innov_ref, prior_ref,
+    list_ref, count_ref, loc_ref, state_ref, obs_hbm, prec_hbm, innov_hbm, prior_hbm,
     out_ref,
-    listed, seen_obs, table, states_in, wide, result, seen, extra, system, diag, vectors, qcol,
+    listed, seen_obs, table, states_in, wide, result, seen, entry_rows, extra, system, diag, vectors, qcol,
     ring_send, ring_recv, obs_send, obs_recv, state_send, state_recv, out_send, out_recv, own_sem,
-    table_send, table_recv,
-    *blocks, side, nb, group,
+    table_send, table_recv, load_sem, obs_ref, given_ref, prior_ref,
+    *blocks, side, nb, sub, group,
 ):
     pieces, mems, entries, part, width = seen_obs.shape
     members_dev, count = obs_ref.shape[:2]
-    rows_space, slots = list_ref.shape
+    slots, rows_space = list_ref.shape
     regions = rows_space // mems
     members = mems * members_dev
     p_size = state_ref.shape[2]
@@ -73,24 +73,33 @@
     def peer(step):
         return (mem + step) % mems
 
+    loads = [
+        pltpu.make_async_copy(obs_hbm, obs_ref, load_sem.at[0]),
+        pltpu.make_async_copy(prec_hbm, given_ref.at[0], load_sem.at[1]),
+        pltpu.make_async_copy(innov_hbm, given_ref.at[1], load_sem.at[2]),
+        pltpu.make_async_copy(prior_hbm, prior_ref, load_sem.at[3]),
+    ]
+    for load in loads:
+        load.start()
     barrier = pltpu.get_barrier_semaphore()
     for there in [at(0, 1, 0), at(0, -1, 0), at(0, 0, 1), at(0, 0, -1)]:
         pl.semaphore_signal(barrier, inc=1, device_id={"space": there, "mem": mem})
     for step in range(1, mems):
         pl.semaphore_signal(barrier, inc=1, device_id={"space": space, "mem": peer(step)})
 
-    for k in range(members_dev):
-        wide[0, k * count : (k + 1) * count, :] = obs_ref[k].astype(F32)
-
-    def turn(b, carry):
-        block = wide[0, pl.ds(b, members_dev, stride=count), :].astype(BF16)
-        for p in range(pieces):
-            blocks[p][space * count + b] = block[p * part : (p + 1) * part]
-        return carry
-
-    lax.fori_loop(0, count, turn, 0, unroll=4)
-    here = pl.ds(pl.multiple_of(space * count, count), count)
-    table[core, here, :] = jnp.where(core == 0, prec_ref[...], innov_ref[...])
+    def turn(p):
+        for k in range(part):
+            wide[0, k * count : (k + 1) * count, :] = obs_ref[p * part + k].astype(F32)
+
+        def one(b, carry):
+            block = wide[0, pl.ds(b, part, stride=count), :].astype(BF16)
+            blocks[p][space * count + b] = block
+            return carry
+
+        lax.fori_loop(0, count, one, 0, unroll=8)
+
+    loads[0].wait()
+    turn(0)
     pl.semaphore_wait(barrier, 4 + mems - 1)
 
     rings = [*blocks, table.at[core]]
@@ -143,6 +152,24 @@
     def begin(p):
         start(p, 0, 1, 4, 5)
 
+    def spread(p):
+        arrive(p, 0)
+        start(p, 2, 8, 9)
+        arrive(p, 1)
+        start(p, 3, 12, 13)
+        arrive(p, 2, 3)
+        start(p, 16, 17)
+
+    def hand_on(p):
+        for j in range(4):
+            for kind in (0, 1):
+                arrive(p, 4 + 4 * j + kind)
+                start(p, 4 + 4 * j + kind + 2)
+
+    def gathered(p):
+        for j in range(4):
+            arrive(p, 6 + 4 * j, 7 + 4 * j)
+
     def state_copy(step):
         to = peer(step)
         return pltpu.make_async_remote_copy(
@@ -176,41 +203,29 @@
         for step in range(1, mems):
             state_copy(step).start()
 
-    sequence = [0, pieces, *range(1, pieces)]
     begin(0)
-    begin_states()
-    for turn_number, p in enumerate(sequence):
-        arrive(p, 0)
-        start(p, 2, 8, 9)
-        arrive(p, 1)
-        start(p, 3, 12, 13)
-        arrive(p, 2, 3)
-        start(p, 16, 17)
-        if turn_number + 1 < len(sequence):
-            begin(sequence[turn_number + 1])
-        for j in range(4):
-            for kind in (0, 1):
-                arrive(p, 4 + 4 * j + kind)
-                start(p, 4 + 4 * j + kind + 2)
-        for j in range(4):
-            arrive(p, 6 + 4 * j, 7 + 4 * j)
-        if p == pieces:
-            other = pltpu.make_async_remote_copy(
-                src_ref=table.at[core],
-                dst_ref=table.at[core],
-                send_sem=table_send,
-                recv_sem=table_recv,
-                device_id={"space": space, "mem": mem + 1 - 2 * core},
-            )
-            other.start()
-            continue
+    for p in range(1, pieces):
+        turn(p)
+    for load in loads[1:]:
+        load.wait()
+    here = pl.ds(pl.multiple_of(space * count, count), count)
+    table[core, here, :] = jnp.where(core == 0, given_ref[0], given_ref[1])
+    spread(0)
+    begin(1)
+    for p in range(pieces):
+        hand_on(p)
+        if p + 1 < pieces:
+            spread(p + 1)
+        if p + 1 < pieces:
+            begin(p + 2 if p + 2 < pieces else pieces)
+        gathered(p)
 
         def pick(r, carry, p=p):
             for l in range(slots):
-                listed[p, r * slots + l] = blocks[p][list_ref[r, l]]
+                listed[p, r * slots + l] = blocks[p][list_ref[l, r]]
             return carry
 
-        lax.fori_loop(0, rows_space, pick, 0)
+        lax.fori_loop(0, rows_space, pick, 0, unroll=4)
         mine = pltpu.make_async_copy(
             listed.at[p, pl.ds(pl.multiple_of(mem * entries, entries), entries)],
             seen_obs.at[p, mem],
@@ -221,6 +236,7 @@
         for step in range(1, mems):
             obs_copy(p, step).start()
 
+    begin_states()
     extra[...] = jnp.zeros_like(extra)
     shares_all = prior_ref[pl.ds(pl.multiple_of(first, regions), regions), :]
     shares_all = shares_all / jnp.sum(shares_all, axis=1, keepdims=True)
@@ -228,25 +244,51 @@
     for r in range(regions):
         qcol[r] = jnp.broadcast_to(root_t[:, r : r + 1], (members, 128))
     halves = members // 128
-    for step in range(1, mems):
-        state_copy(step).wait_recv()
-    local[0].wait()
-    for m in range(mems):
-        many = states_in[m].astype(F32).reshape(members_dev * regions, p_size)
-        for h in range(p_size // 128):
-            wide[h, m * members_dev * regions : (m + 1) * members_dev * regions, :] = many[
-                :, h * 128 : (h + 1) * 128
-            ]
+    spread(pieces)
+    hand_on(pieces)
+    gathered(pieces)
+    other = pltpu.make_async_remote_copy(
+        src_ref=table.at[core],
+        dst_ref=table.at[core],
+        send_sem=table_send,
+        recv_sem=table_recv,
+        device_id={"space": space, "mem": mem + 1 - 2 * core},
+    )
+    other.start()
     other.wait()
+
+    def fetch(r, carry):
+        row = first + r
+        for l in range(slots):
+            block = list_ref[l, row]
+            live = jnp.where(l < count_ref[row], loc_ref[l, row], 0.0)
+            entry_rows[0, pl.ds(r * slots + l, 1), :] = live * table[0, pl.ds(block, 1), :]
+            entry_rows[1, pl.ds(r * slots + l, 1), :] = table[1, pl.ds(block, 1), :]
+        return carry
+
+    lax.fori_loop(0, regions, fetch, 0)
+    entry_rows[0] = jnp.sqrt(entry_rows[0])
+    entry_rows[1] = entry_rows[0] * entry_rows[1]
     for copy in sent:
         copy.wait_send()
-    for step in range(1, mems):
-        state_copy(step).wait_send()
-    for copy in local[1:]:
-        copy.wait()
-    for p in range(pieces):
-        for step in range(1, mems):
-            obs_copy(p, step).wait()
+    for p in range(0, pieces, 2):
+        for which in (p, p + 1):
+            local[which].wait()
+            for step in range(1, mems):
+                obs_copy(which, step).wait()
+
+        def weigh(r, carry, p=p):
+            for l in range(slots):
+                scale = entry_rows[0, pl.ds(r * slots + l, 1), :]
+                for m in range(mems):
+                    picked = jnp.concatenate(
+                        [seen_obs[p, m, r * slots + l], seen_obs[p + 1, m, r * slots + l]], axis=0
+                    ).astype(F32)
+                    at_m = slice(m * members_dev + p * part, m * members_dev + (p + 2) * part)
+                    seen[r, at_m, l * width : (l + 1) * width] = (picked * scale).astype(BF16)
+            return carry
+
+        lax.fori_loop(0, regions, weigh, 0, unroll=2)
 
     row_id = lax.broadcasted_iota(jnp.int32, (members, members), 0)
     col_id = lax.broadcasted_iota(jnp.int32, (members, members), 1)
@@ -256,20 +298,12 @@
         return s / jnp.sum(s, axis=1, keepdims=True)
 
     def build(r, carry):
-        row = first + r
         for l in range(slots):
-            block = list_ref[row, l]
-            live = jnp.where(l < count_ref[row], loc_ref[row, l], 0.0)
-            scale = jnp.sqrt(live * table[0, pl.ds(block, 1), :])
-            picked = jnp.concatenate(
-                [seen_obs[p, m, r * slots + l] for m in range(mems) for p in range(pieces)], axis=0
-            ).astype(F32)
             cols = slice(l * width, (l + 1) * width)
-            seen[:, cols] = (picked * scale).astype(BF16)
-            high, low = split(scale * table[1, pl.ds(block, 1), :])
+            high, low = split(entry_rows[1, pl.ds(r * slots + l, 1), :])
             extra[0:1, cols] = high.astype(F32)
             extra[1:2, cols] = low.astype(F32)
-        all_seen = seen[...]
+        all_seen = seen[r]
         gram = dot(all_seen, all_seen, ((1,), (1,)))
         proj = dot(extra[...].astype(BF16), all_seen, ((1,), (1,)))
         proj = proj[0:1] + proj[1:2]
@@ -288,18 +322,47 @@
 
     lax.fori_loop(0, regions, build, 0, unroll=2)
 
+    def take_states():
+        for step in range(1, mems):
+            state_copy(step).wait()
+        local[-1].wait()
+        for m in range(mems):
+            many = states_in[m].astype(F32).reshape(members_dev * regions, p_size)
+            for h in range(p_size // 128):
+                wide[h, m * members_dev * regions : (m + 1) * members_dev * regions, :] = many[
+                    :, h * 128 : (h + 1) * 128
+                ]
+
     lane_id = lax.broadcasted_iota(jnp.int32, (regions, 128), 1)
     for b in range(members // nb):
         h_b, place = b * nb // 128, b * nb % 128
-        rows = []
-        for i in range(nb):
-            row = system[h_b, pl.ds(b * nb + i, regions, stride=members), :]
-            if place:
-                row = pltpu.roll(row, 128 - place, 1)
-            rows.append(jnp.where(lane_id < nb, row, jnp.where(lane_id == nb + i, 1.0, 0.0)))
-        rows = eliminate(rows, group)
-        for i in range(nb):
-            diag[pl.ds(i, regions, stride=nb), :] = rows[i]
+        if b == members // nb // 2:
+            take_states()
+        for part_b in range(0, nb, sub):
+            if part_b == 0:
+                rows = []
+                for i in range(sub):
+                    row = system[h_b, pl.ds(b * nb + i, regions, stride=members), :]
+                    if place:
+                        row = pltpu.roll(row, 128 - place, 1)
+                    rows.append(jnp.where(lane_id < nb, row, jnp.where(lane_id == nb + i, 1.0, 0.0)))
+            else:
+                rows = [diag[pl.ds(part_b + i, regions, stride=nb), :] for i in range(sub)]
+            rows = eliminate(rows, group, part_b)
+            for i in range(sub):
+                diag[pl.ds(part_b + i, regions, stride=nb), :] = rows[i]
+            if part_b:
+                continue
+            for r in range(regions):
+                ready = diag[r * nb : r * nb + sub, :]
+                later = system[h_b, r * members + b * nb + sub : r * members + (b + 1) * nb, :]
+                if place:
+                    later = pltpu.roll(later, 128 - place, 1)
+                lanes = lax.broadcasted_iota(jnp.int32, (nb - sub, 128), 1)
+                which = lax.broadcasted_iota(jnp.int32, (nb - sub, 128), 0)
+                later = jnp.where(lanes < nb, later, jnp.where(lanes == nb + sub + which, 1.0, 0.0))
+                later = later - dot(ready[:, sub:nb], ready, ((0,), (0,)), HIGHEST)
+                diag[r * nb + sub : (r + 1) * nb, :] = later
 
         def sweep(r, carry, b=b, h_b=h_b, place=place):
             begins = r * members + b * nb
@@ -365,7 +428,7 @@
             out_copy(r, step).start()
         return carry
 
-    lax.fori_loop(0, regions, finish, 0)
+    lax.fori_loop(0, regions, finish, 0, unroll=2)
 
     def close(r, carry):
         own_out(r).wait()
@@ -378,7 +441,7 @@
 
 SMEM = pl.BlockSpec(memory_space=pltpu.SMEM)
 VMEM = pl.BlockSpec(memory_space=pltpu.VMEM)
-ANY = pl.BlockSpec(memory_space=pl.ANY)
+HBM = pl.BlockSpec(memory_space=pltpu.HBM)
 
 
 def body(
@@ -396,8 +459,8 @@
     nb = 64
     dma = pltpu.SemaphoreType.DMA
     updated = pl.pallas_call(
-        functools.partial(whole, side=math.isqrt(spaces), nb=nb, group=8),
-        in_specs=[SMEM, SMEM, SMEM, ANY, VMEM, VMEM, VMEM, VMEM],
+        functools.partial(whole, side=math.isqrt(spaces), nb=nb, sub=32, group=8),
+        in_specs=[SMEM, SMEM, SMEM, HBM, HBM, HBM, HBM, HBM],
         out_specs=VMEM,
         out_shape=jax.ShapeDtypeStruct((regions_dev, members_dev, p_size), BF16),
         scratch_shapes=[
@@ -407,7 +470,8 @@
             pltpu.VMEM((mems, members_dev, regions, p_size), BF16),
             pltpu.VMEM((p_size // 128, max(members * regions, members_dev * blocks_dev), 128), F32),
             pltpu.VMEM((regions, members, p_size), BF16),
-            pltpu.VMEM((members, slots * width), BF16),
+            pltpu.VMEM((regions, members, slots * width), BF16),
+            pltpu.VMEM((2, entries, width), F32),
             pltpu.VMEM((16, slots * width), F32),
             pltpu.VMEM((members // 128, regions * members, 128), F32),
             pltpu.VMEM((regions * nb, 128), F32),
@@ -424,12 +488,19 @@
             dma((pieces + 1,)),
             dma(()),
             dma(()),
+            dma((4,)),
+            pltpu.VMEM((members_dev, blocks_dev, width), BF16),
+            pltpu.VMEM((2, blocks_dev, width), F32),
+            pltpu.VMEM((regions_dev, members), F32),
             *[pltpu.VMEM((blocks_dev * spaces, part, width), BF16) for _ in range(pieces)],
         ],
         compiler_params=pltpu.CompilerParams(
-            vmem_limit_bytes=52 << 20, collective_id=0, has_side_effects=True
+            vmem_limit_bytes=63 << 20, collective_id=0, has_side_effects=True
         ),
-    )(block_list, block_count, loc_weight, ensemble_state, obs_ens, obs_prec, innovation, prior_weight)
+    )(
+        block_list.T, block_count, loc_weight.T,
+        ensemble_state, obs_ens, obs_prec, innovation, prior_weight,
+    )
     return jnp.transpose(updated, (1, 0, 2))
 
 

time: 142 us -> 123 us (0.87)
  Pallas kernels: 136 us -> 120 us
  local copies, waits for them, and re-layouts: 5.7 us -> 2.78 us
    pallas_call x1, Pallas kernels: 136 us -> 120 us  [body(): pl.pallas_call(functools.partial(whole, side=math.isqrt(spaces), nb=nb, s...]
    unnamed x12 -> x0, local copies, waits for them, and re-layouts: 4.14 us -> none
where the time goes in v4:
time: 123 us
  Pallas kernels  120 us (98%)
  local copies, waits for them, and re-layouts  2.78 us (2%)
    pallas_call x1, Pallas kernels, body(): pl.pallas_call(functools.partial(whole, side=math.isqrt(spaces), nb=nb, s...  120 us
    transpose x1, local copies, waits for them, and re-layouts, body(): return jnp.transpose(updated, (1, 0, 2))  2.78 us

profile of v4, /device:TPU:1, one launch (start us, length us, event | category | flops | bytes accessed | tf_op | source)
XLA Modules:
  0.0 122.8 jit_solution(1591057073869183657)
XLA Ops:
  0.0 120.1 %shard_map.82 = bf16[64,32,256]{2,1,0:T(8,128)(2,1)} custom-call(s32[8,64]{1,0:T(8,128)} %bitcast.4, s32[64]{0:T(128)} %count_ref.1, f32[8,64]{1,0:T(8,128)} %bitcast.5, bf16[32,64,256]{2,1,0:T(8,128)(2,1)} %state_ref.1, bf16[32,64,128]{2,1,0:T(8,128)(2,1)} %obs_hbm.1, f32[64,128]{1,0:T(8,128)} %prec_hbm.1, f32[64,128]{1,0:T(8,128)} %innov_hbm.1, ...), custom_call_target="tpu_custom_call" | custom-call | tf_op jit(solution)/shard_map/pallas_call | solution.py:461
  120.1 2.8 %copy.9 = bf16[32,64,256]{2,1,0:T(8,128)(2,1)} copy(bf16[32,64,256]{2,0,1:T(8,128)(2,1)} %bitcast.3) | data formatting | bytes 2097152 | tf_op jit(solution)/shard_map/transpose | solution.py:504

commit v5 on v4

--- a/solution.py
+++ b/solution.py
@@ -49,7 +49,7 @@
 def whole(
     list_ref, count_ref, loc_ref, state_ref, obs_hbm, prec_hbm, innov_hbm, prior_hbm,
     out_ref,
-    listed, seen_obs, table, states_in, wide, result, seen, entry_rows, extra, system, diag, vectors, qcol,
+    listed, seen_obs, table, states_in, wide, result, seen, entry_rows, picked_rows, given_rows, extra, system, diag, vectors, qcol,
     ring_send, ring_recv, obs_send, obs_recv, state_send, state_recv, out_send, out_recv, own_sem,
     table_send, table_recv, load_sem, obs_ref, given_ref, prior_ref,
     *blocks, side, nb, sub, group,
@@ -71,7 +71,7 @@
         return (x + dx + side) % side * side + (z + dz + side) % side
 
     def peer(step):
-        return (mem + step) % mems
+        return (mem // 2 + step // 2) % (mems // 2) * 2 + (core + step % 2) % 2
 
     loads = [
         pltpu.make_async_copy(obs_hbm, obs_ref, load_sem.at[0]),
@@ -102,7 +102,7 @@
     turn(0)
     pl.semaphore_wait(barrier, 4 + mems - 1)
 
-    rings = [*blocks, table.at[core]]
+    rings = [*blocks, table]
 
     def send(p, axis, number, chunk, share, to):
         start, size = {"all": (0, half), "low": (0, half // 2), "high": (half // 2, half // 2)}[share]
@@ -204,12 +204,14 @@
             state_copy(step).start()
 
     begin(0)
+    begin_states()
+    local_states = local.pop()
     for p in range(1, pieces):
         turn(p)
     for load in loads[1:]:
         load.wait()
     here = pl.ds(pl.multiple_of(space * count, count), count)
-    table[core, here, :] = jnp.where(core == 0, given_ref[0], given_ref[1])
+    table[here, :] = jnp.where(core == 0, given_ref[0], given_ref[1])
     spread(0)
     begin(1)
     for p in range(pieces):
@@ -218,14 +220,22 @@
             spread(p + 1)
         if p + 1 < pieces:
             begin(p + 2 if p + 2 < pieces else pieces)
+        else:
+            spread(pieces)
         gathered(p)
 
-        def pick(r, carry, p=p):
-            for l in range(slots):
-                listed[p, r * slots + l] = blocks[p][list_ref[l, r]]
-            return carry
-
-        lax.fori_loop(0, rows_space, pick, 0, unroll=4)
+        for step in sorted(range(mems), key=lambda k: (k == 0, k == 1, k // 2 != mems // 4)):
+            to = peer(step)
+
+            def pick(r, carry, p=p, to=to):
+                row = to * regions + r
+                for l in range(slots):
+                    listed[p, row * slots + l] = blocks[p][list_ref[l, row]]
+                return carry
+
+            lax.fori_loop(0, regions, pick, 0, unroll=4)
+            if step:
+                obs_copy(p, step).start()
         mine = pltpu.make_async_copy(
             listed.at[p, pl.ds(pl.multiple_of(mem * entries, entries), entries)],
             seen_obs.at[p, mem],
@@ -233,10 +243,7 @@
         )
         mine.start()
         local.append(mine)
-        for step in range(1, mems):
-            obs_copy(p, step).start()
-
-    begin_states()
+
     extra[...] = jnp.zeros_like(extra)
     shares_all = prior_ref[pl.ds(pl.multiple_of(first, regions), regions), :]
     shares_all = shares_all / jnp.sum(shares_all, axis=1, keepdims=True)
@@ -244,31 +251,38 @@
     for r in range(regions):
         qcol[r] = jnp.broadcast_to(root_t[:, r : r + 1], (members, 128))
     halves = members // 128
-    spread(pieces)
     hand_on(pieces)
     gathered(pieces)
+    def pick_rows(r, carry):
+        for c in range(2):
+            for l in range(slots):
+                block = list_ref[l, (mem - core + c) * regions + r]
+                picked_rows[c, pl.ds(r * slots + l, 1), :] = table[pl.ds(block, 1), :]
+        return carry
+
+    lax.fori_loop(0, regions, pick_rows, 0, unroll=2)
     other = pltpu.make_async_remote_copy(
-        src_ref=table.at[core],
-        dst_ref=table.at[core],
+        src_ref=picked_rows.at[1 - core],
+        dst_ref=given_rows.at[core],
         send_sem=table_send,
         recv_sem=table_recv,
         device_id={"space": space, "mem": mem + 1 - 2 * core},
     )
     other.start()
+    given_rows[core] = picked_rows[core]
     other.wait()
 
     def fetch(r, carry):
         row = first + r
         for l in range(slots):
-            block = list_ref[l, row]
+            at_e = pl.ds(r * slots + l, 1)
             live = jnp.where(l < count_ref[row], loc_ref[l, row], 0.0)
-            entry_rows[0, pl.ds(r * slots + l, 1), :] = live * table[0, pl.ds(block, 1), :]
-            entry_rows[1, pl.ds(r * slots + l, 1), :] = table[1, pl.ds(block, 1), :]
+            entry_rows[0, at_e, :] = live * given_rows[0, at_e, :]
         return carry
 
     lax.fori_loop(0, regions, fetch, 0)
     entry_rows[0] = jnp.sqrt(entry_rows[0])
-    entry_rows[1] = entry_rows[0] * entry_rows[1]
+    entry_rows[1] = entry_rows[0] * given_rows[1]
     for copy in sent:
         copy.wait_send()
     for p in range(0, pieces, 2):
@@ -320,12 +334,12 @@
         vectors[pl.ds(r, 1), :] = root * (proj - jnp.sum(shares * proj, axis=1, keepdims=True))
         return carry
 
-    lax.fori_loop(0, regions, build, 0, unroll=2)
+    lax.fori_loop(0, regions, build, 0, unroll=4)
 
     def take_states():
         for step in range(1, mems):
             state_copy(step).wait()
-        local[-1].wait()
+        local_states.wait()
         for m in range(mems):
             many = states_in[m].astype(F32).reshape(members_dev * regions, p_size)
             for h in range(p_size // 128):
@@ -428,7 +442,7 @@
             out_copy(r, step).start()
         return carry
 
-    lax.fori_loop(0, regions, finish, 0, unroll=2)
+    lax.fori_loop(0, regions, finish, 0, unroll=4)
 
     def close(r, carry):
         own_out(r).wait()
@@ -466,11 +480,13 @@
         scratch_shapes=[
             pltpu.VMEM((pieces, regions_dev * slots, part, width), BF16),
             pltpu.VMEM((pieces, mems, entries, part, width), BF16),
-            pltpu.VMEM((2, blocks_dev * spaces, width), F32),
+            pltpu.VMEM((blocks_dev * spaces, width), F32),
             pltpu.VMEM((mems, members_dev, regions, p_size), BF16),
             pltpu.VMEM((p_size // 128, max(members * regions, members_dev * blocks_dev), 128), F32),
             pltpu.VMEM((regions, members, p_size), BF16),
             pltpu.VMEM((regions, members, slots * width), BF16),
+            pltpu.VMEM((2, entries, width), F32),
+            pltpu.VMEM((2, entries, width), F32),
             pltpu.VMEM((2, entries, width), F32),
             pltpu.VMEM((16, slots * width), F32),
             pltpu.VMEM((members // 128, regions * members, 128), F32),

time: 123 us -> 119 us (0.967)
  Pallas kernels: 120 us -> 116 us
    pallas_call x1, Pallas kernels: 120 us -> 116 us  [body(): pl.pallas_call(functools.partial(whole, side=math.isqrt(spaces), nb=nb, s...]
where the time goes in v5:
time: 119 us
  Pallas kernels  116 us (97%)
  local copies, waits for them, and re-layouts  2.78 us (2%)
    pallas_call x1, Pallas kernels, body(): pl.pallas_call(functools.partial(whole, side=math.isqrt(spaces), nb=nb, s...  116 us
    transpose x1, local copies, waits for them, and re-layouts, body(): return jnp.transpose(updated, (1, 0, 2))  2.78 us

profile of v5, /device:TPU:1, one launch (start us, length us, event | category | flops | bytes accessed | tf_op | source)
XLA Modules:
  0.0 118.8 jit_solution(13037007458770439614)
XLA Ops:
  0.0 116.0 %shard_map.82 = bf16[64,32,256]{2,1,0:T(8,128)(2,1)} custom-call(s32[8,64]{1,0:T(8,128)} %bitcast.4, s32[64]{0:T(128)} %count_ref.1, f32[8,64]{1,0:T(8,128)} %bitcast.5, bf16[32,64,256]{2,1,0:T(8,128)(2,1)} %state_ref.1, bf16[32,64,128]{2,1,0:T(8,128)(2,1)} %obs_hbm.1, f32[64,128]{1,0:T(8,128)} %prec_hbm.1, f32[64,128]{1,0:T(8,128)} %innov_hbm.1, ...), custom_call_target="tpu_custom_call" | custom-call | tf_op jit(solution)/shard_map/pallas_call | solution.py:475
  116.0 2.8 %copy.9 = bf16[32,64,256]{2,1,0:T(8,128)(2,1)} copy(bf16[32,64,256]{2,0,1:T(8,128)(2,1)} %bitcast.3) | data formatting | bytes 2097152 | tf_op jit(solution)/shard_map/transpose | solution.py:520

commit v6 on v5

--- a/solution.py
+++ b/solution.py
@@ -302,7 +302,8 @@
                     seen[r, at_m, l * width : (l + 1) * width] = (picked * scale).astype(BF16)
             return carry
 
-        lax.fori_loop(0, regions, weigh, 0, unroll=2)
+        if p + 2 < pieces:
+            lax.fori_loop(0, regions, weigh, 0, unroll=2)
 
     row_id = lax.broadcasted_iota(jnp.int32, (members, members), 0)
     col_id = lax.broadcasted_iota(jnp.int32, (members, members), 1)
@@ -312,6 +313,7 @@
         return s / jnp.sum(s, axis=1, keepdims=True)
 
     def build(r, carry):
+        weigh(r, carry)
         for l in range(slots):
             cols = slice(l * width, (l + 1) * width)
             high, low = split(entry_rows[1, pl.ds(r * slots + l, 1), :])
@@ -334,7 +336,7 @@
         vectors[pl.ds(r, 1), :] = root * (proj - jnp.sum(shares * proj, axis=1, keepdims=True))
         return carry
 
-    lax.fori_loop(0, regions, build, 0, unroll=4)
+    lax.fori_loop(0, regions, build, 0, unroll=True)
 
     def take_states():
         for step in range(1, mems):

time: 119 us -> 118 us (level)
  no operation moved by 1% of the time
where the time goes in v6:
time: 118 us
  Pallas kernels  115 us (97%)
  local copies, waits for them, and re-layouts  2.78 us (2%)
    pallas_call x1, Pallas kernels, body(): pl.pallas_call(functools.partial(whole, side=math.isqrt(spaces), nb=nb, s...  115 us
    transpose x1, local copies, waits for them, and re-layouts, body(): return jnp.transpose(updated, (1, 0, 2))  2.78 us

profile of v6, /device:TPU:1, one launch (start us, length us, event | category | flops | bytes accessed | tf_op | source)
XLA Modules:
  0.0 118.1 jit_solution(7855297430732211623)
XLA Ops:
  0.0 115.3 %shard_map.82 = bf16[64,32,256]{2,1,0:T(8,128)(2,1)} custom-call(s32[8,64]{1,0:T(8,128)} %bitcast.4, s32[64]{0:T(128)} %count_ref.1, f32[8,64]{1,0:T(8,128)} %bitcast.5, bf16[32,64,256]{2,1,0:T(8,128)(2,1)} %state_ref.1, bf16[32,64,128]{2,1,0:T(8,128)(2,1)} %obs_hbm.1, f32[64,128]{1,0:T(8,128)} %prec_hbm.1, f32[64,128]{1,0:T(8,128)} %innov_hbm.1, ...), custom_call_target="tpu_custom_call" | custom-call | tf_op jit(solution)/shard_map/pallas_call | solution.py:477
  115.4 2.8 %copy.9 = bf16[32,64,256]{2,1,0:T(8,128)(2,1)} copy(bf16[32,64,256]{2,0,1:T(8,128)(2,1)} %bitcast.3) | data formatting | bytes 2097152 | tf_op jit(solution)/shard_map/transpose | solution.py:522
